TPU v7x, 32 devices: a whole 2x2x4 slice. The times are simulated.
32 devices in a mesh: member: 4 (over y, x), lat: 8 (over z, core).
Axes of the slice: x: 2, y: 2, z: 4, core: 2. Of those that a mesh axis runs over, the one named last changes fastest.
Arguments:
- initial_states: float32 [4, 16, 80, 128], P('member', 'lat'), may hold values from -6 to 6
- targets: float32 [2, 16, 80, 128], P(None, 'lat'), may hold values from -6 to 6
- lat_weight: float32 [16], P('lat'), may hold values from 0.3 to 3
- weight_in: float32 [256, 720], replicated, may hold values from -0.21875 to 0.21875
- weight_out: float32 [80, 2304], replicated, may hold values from -0.125 to 0.125
- hidden_bias: float32 [256], replicated, may hold values from -4 to 4
Outputs:
- state_grad: float32 [4, 16, 80, 128], P('member', 'lat')
- loss: float32 [], replicated
All inputs are finite; a program needn't handle non-finite values.
Results may differ from a plain program's by a relative error of at most 0.00023.
Values sent between devices are 32-bit elements; how exact they have to be, the bound alone decides.
A program may use at most 64 MiB of HBM per device.

v0:
```python
import functools

import jax
import jax.numpy as jnp
from jax import lax
from jax.experimental import pallas as pl
from jax.experimental.pallas import tpu as pltpu
from jax.sharding import PartitionSpec as P

smooth_width = 0.1
gelu_scale = 0.7978845608028654
gelu_cubic = 0.044715
MESH = pl.DeviceIdType.MESH
F32 = jnp.float32
BF16 = jnp.bfloat16


def split(value):
    high = value.astype(BF16)
    low = (value - high.astype(F32)).astype(BF16)
    return high, low


def shifted(value, tap):
    if tap == 1:
        return value
    columns = value.shape[-1]
    lane = lax.broadcasted_iota(jnp.int32, value.shape, 1)
    if tap == 0:
        return jnp.where(lane == 0, 0.0, pltpu.roll(value, 1, 1))
    return jnp.where(lane == columns - 1, 0.0, pltpu.roll(value, columns - 1, 1))


def dot(left, right):
    return jnp.dot(left, right, preferred_element_type=F32)


def kernel(
    members, bands,
    x_hbm, target_hbm, lat_hbm, w_in_hbm, w_out_hbm, bias_hbm,
    grad_ref, loss_ref,
    x_ref, target_ref, lat_ref, w_in_ref, w_out_ref, bias_ref, fetch_sem,
    halo, others, parts_m, parts_l, fields, grads, part_src,
    win, winb, wout, woutb, tall, s_high, s_low, h_high, h_low, before, slope, loss_grad, bias,
    halo_send, halo_recv, other_send, other_recv, pm_send, pm_recv, pl_send, pl_recv,
):
    steps, rows, chans, cols = target_ref.shape
    hidden = w_in_ref.shape[1]
    taps = 3 * chans
    depth = win.shape[2]
    deep = 3 * hidden
    me_m = lax.axis_index("member")
    me_l = lax.axis_index("lat")
    has_up = me_l > 0
    has_down = me_l < bands - 1

    fetches = [
        pltpu.make_async_copy(source, target, fetch_sem.at[n])
        for n, (source, target) in enumerate([
            (x_hbm, x_ref), (w_in_hbm, w_in_ref), (w_out_hbm, w_out_ref),
            (bias_hbm, bias_ref), (target_hbm, target_ref), (lat_hbm, lat_ref)])
    ]
    barrier = pltpu.get_barrier_semaphore()
    for k in range(1, members):
        pl.semaphore_signal(barrier, inc=1, device_id={"member": lax.rem(me_m + k, members)}, device_id_type=MESH)
    for k in range(1, bands):
        pl.semaphore_signal(barrier, inc=1, device_id={"lat": lax.rem(me_l + k, bands)}, device_id_type=MESH)

    for fetch in fetches:
        fetch.start()

    @pl.when(jnp.logical_not(has_up))
    def _():
        for n in range(2 * steps):
            halo[n, 0] = jnp.zeros(halo.shape[2:], F32)

    @pl.when(jnp.logical_not(has_down))
    def _():
        for n in range(2 * steps):
            halo[n, 1] = jnp.zeros(halo.shape[2:], F32)

    def to_up(n, source):
        return pltpu.make_async_remote_copy(
            src_ref=source.at[0:2], dst_ref=halo.at[n, 1],
            send_sem=halo_send.at[n, 0], recv_sem=halo_recv.at[n, 1],
            device_id={"lat": jnp.maximum(me_l - 1, 0)}, device_id_type=MESH)

    def to_down(n, source):
        return pltpu.make_async_remote_copy(
            src_ref=source.at[rows - 2:rows], dst_ref=halo.at[n, 0],
            send_sem=halo_send.at[n, 1], recv_sem=halo_recv.at[n, 0],
            device_id={"lat": jnp.minimum(me_l + 1, bands - 1)}, device_id_type=MESH)

    def halo_start(n, source):
        @pl.when(has_up)
        def _():
            to_up(n, source).start()

        @pl.when(has_down)
        def _():
            to_down(n, source).start()

    def halo_wait(n, source):
        @pl.when(has_up)
        def _():
            to_up(n, source).wait_send()
            to_down(n, source).wait_recv()

        @pl.when(has_down)
        def _():
            to_down(n, source).wait_send()
            to_up(n, source).wait_recv()

    def to_member(step, k):
        return pltpu.make_async_remote_copy(
            src_ref=fields.at[step], dst_ref=others.at[step, k - 1],
            send_sem=other_send.at[step, k - 1], recv_sem=other_recv.at[step, k - 1],
            device_id={"member": lax.rem(me_m + k, members)}, device_id_type=MESH)

    fetches[0].wait()
    pl.semaphore_wait(barrier, members + bands - 2)
    halo_start(0, x_ref)

    def put_wide(target, a, block):
        tall[0:taps, :] = block
        high, low = split(tall[...].T)
        target[a, 0:hidden] = high
        target[a, hidden:2 * hidden] = low

    def front_weights():
        for fetch in fetches[1:]:
            fetch.wait()
        tall[taps:, :] = jnp.zeros((depth - taps, hidden), F32)
        for a in range(3):
            put_wide(win, a, w_in_ref[a * taps:(a + 1) * taps, :])
        bias[...] = jnp.broadcast_to(bias_ref[...], (cols, hidden)).T
        for j in range(rows + 4):
            s_high[j * depth + taps:(j + 1) * depth, :] = jnp.zeros((depth - taps, cols), BF16)
            s_low[j * depth + taps:(j + 1) * depth, :] = jnp.zeros((depth - taps, cols), BF16)

    def narrow_weights():
        for a in range(3):
            for b in range(3):
                at = (3 * a + b) * hidden
                high, low = split(w_out_ref[:, at:at + hidden])
                wout[b * chans:(b + 1) * chans, a * hidden:(a + 1) * hidden] = high
                wout[taps + b * chans:taps + (b + 1) * chans, a * hidden:(a + 1) * hidden] = low

    def back_weights():
        for a in range(3):
            for b in range(3):
                at = (3 * (2 - a) + 2 - b) * chans
                high, low = split(w_in_ref[at:at + chans, :])
                winb[b * chans:(b + 1) * chans, a * hidden:(a + 1) * hidden] = high
                winb[taps + b * chans:taps + (b + 1) * chans, a * hidden:(a + 1) * hidden] = low
        for a in range(3):
            at = 3 * (2 - a) * hidden
            put_wide(woutb, a, jnp.concatenate(
                [w_out_ref[:, at + (2 - b) * hidden:at + (3 - b) * hidden] for b in range(3)], axis=0))

    def put_line(i, line):
        for b in range(3):
            high, low = split(shifted(line, b))
            at = i * depth + b * chans
            s_high[at:at + chans, :] = high
            s_low[at:at + chans, :] = low

    def widen_part(weights, inside):
        sums = {}
        for a in range(3):
            lines = [j for j in range(rows + 2) if (2 <= j + a < rows + 2) == inside]
            high = jnp.concatenate([s_high[(j + a) * depth:(j + a + 1) * depth, :] for j in lines], axis=1)
            low = jnp.concatenate([s_low[(j + a) * depth:(j + a + 1) * depth, :] for j in lines], axis=1)
            both = dot(weights[a], high)
            total = both[0:hidden] + both[hidden:2 * hidden] + dot(weights[a, 0:hidden, :], low)
            for n, j in enumerate(lines):
                line = total[:, n * cols:(n + 1) * cols]
                sums[j] = line if j not in sums else sums[j] + line
        return sums

    def widen_own(weights, own):
        for r in range(rows):
            put_line(r + 2, own[r])
        for j, line in widen_part(weights, True).items():
            before[:, j * cols:(j + 1) * cols] = line

    def widen_rest(weights, n):
        for j in range(2):
            put_line(j, halo[n, 0, j])
            put_line(rows + 2 + j, halo[n, 1, j])
        for j, line in widen_part(weights, False).items():
            before[:, j * cols:(j + 1) * cols] += line

    def narrow(weights):
        right = jnp.concatenate([h_high[r * hidden:r * hidden + deep, :] for r in range(rows)], axis=1)
        both = dot(weights[...], right)
        right = jnp.concatenate([h_low[r * hidden:r * hidden + deep, :] for r in range(rows)], axis=1)
        total = both[0:taps] + both[taps:2 * taps] + dot(weights[0:taps, :], right)
        result = []
        for r in range(rows):
            line = total[:, r * cols:(r + 1) * cols]
            result.append(sum(shifted(line[b * chans:(b + 1) * chans], b) for b in range(3)))
        return result

    def put_hidden(j, value):
        if j == 0:
            value = jnp.where(has_up, value, 0.0)
        if j == rows + 1:
            value = jnp.where(has_down, value, 0.0)
        high, low = split(value)
        h_high[j * hidden:(j + 1) * hidden, :] = high
        h_low[j * hidden:(j + 1) * hidden, :] = low

    def fold(value):
        return sum(value[8 * i:8 * i + 8] for i in range(chans // 8))

    def loss_terms(step):
        partial = jnp.zeros((8, cols), F32)
        for r in range(rows):
            weight = lat_ref[0:1, r:r + 1]
            mine = fields[step, r]
            error = mine - target_ref[step, r]
            square = error * error + smooth_width * smooth_width
            inverse = lax.rsqrt(square)
            direct = square * inverse
            gradient = error * inverse
            summed = jnp.full(mine.shape, smooth_width, F32)
            slopes = jnp.zeros_like(mine)
            for k in range(1, members):
                spread = mine - others[step, k - 1, r]
                square = spread * spread + smooth_width * smooth_width
                inverse = lax.rsqrt(square)
                summed = summed + square * inverse
                slopes = slopes + spread * inverse
            partial = partial + weight * fold(direct - summed / (2.0 * (members - 1)))
            loss_grad[step, r] = weight * (gradient - slopes / (members - 1))
        return partial

    for step in range(steps):
        own = x_ref if step == 0 else fields.at[step - 1]
        if step == 0:
            front_weights()
        widen_own(win, own)
        if step == 0:
            narrow_weights()
        halo_wait(step, own)
        widen_rest(win, step)
        for j in range(rows + 2):
            value = before[:, j * cols:(j + 1) * cols] + bias[...]
            inner = jnp.tanh(gelu_scale * (value + gelu_cubic * value * value * value))
            put_hidden(j, 0.5 * value * (1.0 + inner))
            slope[step, :, j * cols:(j + 1) * cols] = 0.5 * (1.0 + inner) + 0.5 * value * (1.0 - inner * inner) * (
                gelu_scale * (1.0 + 3.0 * gelu_cubic * value * value))
        change = narrow(wout)
        for r in range(rows):
            fields[step, r] = own[r] + change[r]
        if step < steps - 1:
            halo_start(step + 1, fields.at[step])
        for k in range(1, members):
            to_member(step, k).start()
        if step == 0:
            back_weights()

    partial = jnp.zeros((8, cols), F32)
    for step in range(steps):
        for k in range(1, members):
            to_member(step, k).wait()
        partial = partial + loss_terms(step)

    def part_to_member(k):
        return pltpu.make_async_remote_copy(
            src_ref=part_src.at[0], dst_ref=parts_m.at[me_m],
            send_sem=pm_send.at[k - 1], recv_sem=pm_recv.at[me_m],
            device_id={"member": lax.rem(me_m + k, members)}, device_id_type=MESH)

    def part_from_member(k):
        source = lax.rem(me_m + k, members)
        return pltpu.make_async_remote_copy(
            src_ref=part_src.at[0], dst_ref=parts_m.at[source],
            send_sem=pm_send.at[k - 1], recv_sem=pm_recv.at[source],
            device_id={"member": source}, device_id_type=MESH)

    def part_to_band(k):
        return pltpu.make_async_remote_copy(
            src_ref=part_src.at[1], dst_ref=parts_l.at[me_l],
            send_sem=pl_send.at[k - 1], recv_sem=pl_recv.at[me_l],
            device_id={"lat": lax.rem(me_l + k, bands)}, device_id_type=MESH)

    def part_from_band(k):
        source = lax.rem(me_l + k, bands)
        return pltpu.make_async_remote_copy(
            src_ref=part_src.at[1], dst_ref=parts_l.at[source],
            send_sem=pl_send.at[k - 1], recv_sem=pl_recv.at[source],
            device_id={"lat": source}, device_id_type=MESH)

    part_src[0] = partial

    for step in range(steps - 1, -1, -1):
        n = 2 * steps - 1 - step
        own = grads.at[step]
        for r in range(rows):
            if step == steps - 1:
                grads[step, r] = loss_grad[step, r]
            else:
                grads[step, r] = grads[step + 1, r] + change[r] + loss_grad[step, r]
        halo_start(n, own)
        if step == steps - 1:
            for k in range(1, members):
                part_to_member(k).start()
            parts_m[me_m] = partial
        else:
            if step == steps - 2:
                for k in range(1, members):
                    part_to_member(k).wait_send()
                    part_from_member(k).wait_recv()
                total = sum(parts_m[k] for k in range(members))
                part_src[1] = total
                for k in range(1, bands):
                    part_to_band(k).start()
                parts_l[me_l] = total
        widen_own(woutb, own)
        halo_wait(n, own)
        widen_rest(woutb, n)
        for j in range(rows + 2):
            put_hidden(j, before[:, j * cols:(j + 1) * cols] * slope[step, :, j * cols:(j + 1) * cols])
        change = narrow(winb)

    for r in range(rows):
        grad_ref[r] = grads[0, r] + change[r]
    for k in range(1, bands):
        part_to_band(k).wait_send()
        part_from_band(k).wait_recv()
    total = sum(parts_l[k] for k in range(bands))
    count = members * steps * rows * bands * chans * cols
    loss_ref[0, 0] = jnp.sum(total) / count


def on_device(members, bands, initial_states, targets, lat_weight, weight_in, weight_out, hidden_bias):
    steps, rows, chans, cols = targets.shape
    hidden = weight_in.shape[0]
    taps = 3 * chans
    depth = -(-taps // 256) * 256
    deep = 3 * hidden
    vmem = pl.BlockSpec(memory_space=pltpu.VMEM)
    smem = pl.BlockSpec(memory_space=pltpu.SMEM)
    dma = pltpu.SemaphoreType.DMA
    gradient, loss = pl.pallas_call(
        functools.partial(kernel, members, bands),
        out_shape=(jax.ShapeDtypeStruct((rows, chans, cols), F32), jax.ShapeDtypeStruct((1, 1), F32)),
        in_specs=[pl.BlockSpec(memory_space=pl.ANY)] * 6,
        out_specs=(vmem, smem),
        scratch_shapes=[
            pltpu.VMEM((rows, chans, cols), F32),
            pltpu.VMEM(targets.shape, F32),
            pltpu.VMEM((1, rows), F32),
            pltpu.VMEM((3 * taps, hidden), F32),
            pltpu.VMEM((chans, 3 * deep), F32),
            pltpu.VMEM((1, hidden), F32),
            dma((6,)),
            pltpu.VMEM((2 * steps, 2, 2, chans, cols), F32),
            pltpu.VMEM((steps, members - 1, rows, chans, cols), F32),
            pltpu.VMEM((members, 8, cols), F32),
            pltpu.VMEM((bands, 8, cols), F32),
            pltpu.VMEM((steps, rows, chans, cols), F32),
            pltpu.VMEM((steps, rows, chans, cols), F32),
            pltpu.VMEM((2, 8, cols), F32),
            pltpu.VMEM((3, 2 * hidden, depth), BF16),
            pltpu.VMEM((2 * taps, deep), BF16),
            pltpu.VMEM((2 * taps, deep), BF16),
            pltpu.VMEM((3, 2 * hidden, depth), BF16),
            pltpu.VMEM((depth, hidden), F32),
            pltpu.VMEM(((rows + 4) * depth, cols), BF16),
            pltpu.VMEM(((rows + 4) * depth, cols), BF16),
            pltpu.VMEM(((rows + 2) * hidden, cols), BF16),
            pltpu.VMEM(((rows + 2) * hidden, cols), BF16),
            pltpu.VMEM((hidden, (rows + 2) * cols), F32),
            pltpu.VMEM((steps, hidden, (rows + 2) * cols), F32),
            pltpu.VMEM((steps, rows, chans, cols), F32),
            pltpu.VMEM((hidden, cols), F32),
            dma((2 * steps, 2)), dma((2 * steps, 2)),
            dma((steps, members - 1)), dma((steps, members - 1)),
            dma((members - 1,)), dma((members,)),
            dma((bands - 1,)), dma((bands,)),
        ],
        compiler_params=pltpu.CompilerParams(collective_id=0, has_side_effects=True),
    )(
        initial_states.reshape(rows, chans, cols), targets, lat_weight.reshape(1, rows),
        weight_in.T, weight_out, hidden_bias.reshape(1, hidden),
    )
    return gradient.reshape(initial_states.shape), loss.reshape(())


def solution(mesh):
    placed = (P("member", "lat", None, None), P(None, "lat", None, None), P("lat"), P(), P(), P())
    return jax.shard_map(
        functools.partial(on_device, mesh.shape["member"], mesh.shape["lat"]),
        mesh=mesh,
        in_specs=placed,
        out_specs=(P("member", "lat", None, None), P()),
        check_vma=False,
    )
```

profile of v0, /device:TPU:1, one launch (start us, length us, event | category | flops | bytes accessed | tf_op | source)
XLA Modules:
  0.0 33.0 jit_solution(12750036125039101865)
XLA Ops:
  0.6 29.1 %shard_map.77 = (f32[2,80,128]{2,1,0:T(8,128)}, f32[1,1]{1,0:T(1,128)}) custom-call(f32[2,80,128]{2,1,0:T(8,128)} %bitcast.7, f32[2,2,80,128]{3,2,1,0:T(8,128)} %target_hbm.1, f32[1,2]{1,0:T(1,128)} %bitcast.10, f32[720,256]{1,0:T(8,128)} %bitcast.6, f32[80,2304]{1,0:T(8,128)} %w_out_hbm.1, f32[1,256]{1,0:T(1,128)} %bitcast.9), custom_call_target="tpu_custom_call" | custom-call | tf_op jit(solution)/shard_map/pallas_call | solution.py:347
  29.8 1.5 %copy.10 = f32[1,2,80,128]{3,2,1,0:T(8,128)} copy(f32[1,2,80,128]{3,2,1,0:T(8,128)} %bitcast.8) | data formatting | bytes 163840
where the time goes:
time: 33.3 us; the launch traced here: 33 us
  Pallas kernels  29.1 us (87%)
  between operations  2.33 us (7%)
  local copies, waits for them, and re-layouts  1.53 us (5%)
    pallas_call x1, Pallas kernels, on_device(): pl.pallas_call(functools.partial(kernel, members, bands), out_shape=(jax....  29.1 us
    unnamed x1, local copies, waits for them, and re-layouts  1.53 us

commit v1 on v0

--- a/solution.py
+++ b/solution.py
@@ -332,7 +332,17 @@
         part_from_band(k).wait_recv()
     total = sum(parts_l[k] for k in range(bands))
     count = members * steps * rows * bands * chans * cols
-    loss_ref[0, 0] = jnp.sum(total) / count
+    loss_ref[...] = jnp.full(loss_ref.shape, jnp.sum(total) / count, F32)
+
+
+def deliver(grad_vmem, loss_vmem, grad_hbm, loss_hbm, loss_smem, sem):
+    gradient = pltpu.make_async_copy(grad_vmem, grad_hbm, sem.at[0])
+    loss = pltpu.make_async_copy(loss_smem, loss_hbm, sem.at[1])
+    gradient.start()
+    loss_smem[0, 0] = loss_vmem[0, 0]
+    loss.start()
+    loss.wait()
+    gradient.wait()
 
 
 def on_device(members, bands, initial_states, targets, lat_weight, weight_in, weight_out, hidden_bias):
@@ -342,13 +352,12 @@
     depth = -(-taps // 256) * 256
     deep = 3 * hidden
     vmem = pl.BlockSpec(memory_space=pltpu.VMEM)
-    smem = pl.BlockSpec(memory_space=pltpu.SMEM)
     dma = pltpu.SemaphoreType.DMA
     gradient, loss = pl.pallas_call(
         functools.partial(kernel, members, bands),
-        out_shape=(jax.ShapeDtypeStruct((rows, chans, cols), F32), jax.ShapeDtypeStruct((1, 1), F32)),
-        in_specs=[pl.BlockSpec(memory_space=pl.ANY)] * 6,
-        out_specs=(vmem, smem),
+        out_shape=(pltpu.VMEM((rows, chans, cols), F32), pltpu.VMEM((8, cols), F32)),
+        in_specs=[pl.BlockSpec(memory_space=pltpu.HBM)] * 6,
+        out_specs=(vmem, vmem),
         scratch_shapes=[
             pltpu.VMEM((rows, chans, cols), F32),
             pltpu.VMEM(targets.shape, F32),
@@ -382,11 +391,20 @@
             dma((members - 1,)), dma((members,)),
             dma((bands - 1,)), dma((bands,)),
         ],
-        compiler_params=pltpu.CompilerParams(collective_id=0, has_side_effects=True),
+        compiler_params=pltpu.CompilerParams(collective_id=0, has_side_effects=True, vmem_limit_bytes=24 * 2**20),
     )(
-        initial_states.reshape(rows, chans, cols), targets, lat_weight.reshape(1, rows),
-        weight_in.T, weight_out, hidden_bias.reshape(1, hidden),
+        *(pltpu.with_memory_space_constraint(value, pltpu.HBM) for value in (
+            initial_states.reshape(rows, chans, cols), targets, lat_weight.reshape(1, rows),
+            weight_in.T, weight_out, hidden_bias.reshape(1, hidden)))
     )
+    anywhere = pl.BlockSpec(memory_space=pl.ANY)
+    gradient, loss = pl.pallas_call(
+        deliver,
+        out_shape=(jax.ShapeDtypeStruct((rows, chans, cols), F32), jax.ShapeDtypeStruct((1, 1), F32)),
+        in_specs=[vmem, vmem],
+        out_specs=(anywhere, anywhere),
+        scratch_shapes=[pltpu.SMEM((1, 1), F32), dma((2,))],
+    )(*(pltpu.with_memory_space_constraint(value, pltpu.VMEM) for value in (gradient, loss)))
     return gradient.reshape(initial_states.shape), loss.reshape(())
 
 

time: 33.3 us -> 30.2 us (0.907)
  between operations: 2.33 us -> 0.64 us
  local copies, waits for them, and re-layouts: 1.53 us -> 0 us
    unnamed x1 -> x0, local copies, waits for them, and re-layouts: 1.53 us -> none
    pallas_call x1 -> x2, Pallas kernels: 29.1 us -> 29.3 us  [the longest x1 28.6 us: on_device(): pl.pallas_call(functools.partial(kernel, members, bands), out_shape=(pltp...]
where the time goes in v1:
time: 30.2 us; the launch traced here: 29.9 us
  Pallas kernels  29.3 us (97%)
  between operations  0.64 us (2%)
    pallas_call x1, Pallas kernels, on_device(): pl.pallas_call(functools.partial(kernel, members, bands), out_shape=(pltp...  28.6 us
    pallas_call x1, Pallas kernels, on_device(): pl.pallas_call(deliver, out_shape=(jax.ShapeDtypeStruct((rows, chans, col...  0.66 us

profile of v1, /device:TPU:1, one launch (start us, length us, event | category | flops | bytes accessed | tf_op | source)
XLA Modules:
  0.0 29.9 jit_solution(1719652881715308345)
XLA Ops:
  0.6 28.6 %shard_map.77 = (f32[2,80,128]{2,1,0:T(8,128)S(1)}, f32[8,128]{1,0:T(8,128)S(1)}) custom-call(f32[2,80,128]{2,1,0:T(8,128)} %bitcast.7, f32[2,2,80,128]{3,2,1,0:T(8,128)} %target_hbm.1, f32[1,2]{1,0:T(1,128)} %bitcast.9, f32[720,256]{1,0:T(8,128)} %bitcast.6, f32[80,2304]{1,0:T(8,128)} %w_out_hbm.1, f32[1,256]{1,0:T(1,128)} %bitcast.8), custom_call_target="tpu_custom_call" | custom-call | tf_op jit(solution)/shard_map/pallas_call | solution.py:356
  29.3 0.7 %shard_map.78 = (f32[2,80,128]{2,1,0:T(8,128)}, f32[1,1]{1,0:T(1,128)}) custom-call(f32[2,80,128]{2,1,0:T(8,128)S(1)} %get-tuple-element.6.grad_vmem, f32[8,128]{1,0:T(8,128)S(1)} %get-tuple-element.7.loss_vmem), custom_call_target="tpu_custom_call" | custom-call | tf_op jit(solution)/shard_map/pallas_call | solution.py:401

commit v2 on v1

v2 whole, which is shorter than its diff:
```python
import functools

import jax
import jax.numpy as jnp
from jax import lax
from jax.experimental import pallas as pl
from jax.experimental.pallas import tpu as pltpu
from jax.sharding import PartitionSpec as P

smooth_width = 0.1
gelu_scale = 0.7978845608028654
gelu_cubic = 0.044715
MESH = pl.DeviceIdType.MESH
F32 = jnp.float32
BF16 = jnp.bfloat16


def split(value):
    high = value.astype(BF16)
    low = (value - high.astype(F32)).astype(BF16)
    return high, low


def shifted(value, tap):
    if tap == 1:
        return value
    columns = value.shape[-1]
    lane = lax.broadcasted_iota(jnp.int32, value.shape, 1)
    if tap == 0:
        return jnp.where(lane == 0, 0.0, pltpu.roll(value, 1, 1))
    return jnp.where(lane == columns - 1, 0.0, pltpu.roll(value, columns - 1, 1))


def dot(left, right):
    return jnp.dot(left, right, preferred_element_type=F32)


def kernel(
    members, bands,
    x_hbm, target_hbm, lat_hbm, w_in_hbm, w_out_hbm, bias_hbm,
    grad_ref, loss_ref,
    x_ref, target_ref, lat_ref, w_in_ref, w_out_ref, bias_ref, fetch_sem,
    halo, others, parts_m, parts_l, fields, grads, part_src,
    win, winb, wout, woutb, tall, s_high, s_low, h_high, h_low, before, slope, narrowed, loss_grad, bias,
    halo_send, halo_recv, other_send, other_recv, pm_send, pm_recv, pl_send, pl_recv,
):
    steps, rows, chans, cols = target_ref.shape
    hidden = w_in_ref.shape[1]
    taps = 3 * chans
    depth = win.shape[2]
    me_m = lax.axis_index("member")
    me_l = lax.axis_index("lat")
    odd = lax.rem(me_l, 2)
    slow = me_l - 1 + 2 * odd
    fast = me_l + 1 - 2 * odd
    has_slow = jnp.logical_and(slow >= 0, slow < bands)
    slow = jnp.clip(slow, 0, bands - 1)

    def mirrored(n, last):
        return n + odd * (last - 2 * n)

    fetches = [
        pltpu.make_async_copy(source, target, fetch_sem.at[n])
        for n, (source, target) in enumerate(
            [(x_hbm.at[mirrored(i, rows - 1)], x_ref.at[i]) for i in range(rows)]
            + [(w_in_hbm, w_in_ref), (w_out_hbm, w_out_ref), (bias_hbm, bias_ref), (lat_hbm, lat_ref)]
            + [(target_hbm.at[:, mirrored(i, rows - 1)], target_ref.at[:, i]) for i in range(rows)])
    ]
    barrier = pltpu.get_barrier_semaphore()
    for k in range(1, members):
        pl.semaphore_signal(barrier, inc=1, device_id={"member": lax.rem(me_m + k, members)}, device_id_type=MESH)
    for k in range(1, bands):
        pl.semaphore_signal(barrier, inc=1, device_id={"lat": lax.rem(me_l + k, bands)}, device_id_type=MESH)

    for fetch in fetches:
        fetch.start()

    @pl.when(jnp.logical_not(has_slow))
    def _():
        for n in range(2 * steps):
            halo[n, 0] = jnp.zeros(halo.shape[2:], F32)

    def to_slow(n, source, far):
        return pltpu.make_async_remote_copy(
            src_ref=source.at[far], dst_ref=halo.at[n, 0, far],
            send_sem=halo_send.at[n, 0, far], recv_sem=halo_recv.at[n, 0, far],
            device_id={"lat": slow}, device_id_type=MESH)

    def to_fast(n, source, far):
        return pltpu.make_async_remote_copy(
            src_ref=source.at[rows - 1 - far], dst_ref=halo.at[n, 1, far],
            send_sem=halo_send.at[n, 1, far], recv_sem=halo_recv.at[n, 1, far],
            device_id={"lat": fast}, device_id_type=MESH)

    def slow_start(n, source, fars=(0, 1)):
        @pl.when(has_slow)
        def _():
            for far in fars:
                to_slow(n, source, far).start()

    def slow_wait(n, source, far):
        @pl.when(has_slow)
        def _():
            to_slow(n, source, far).wait_recv()

    def halo_start(n, source):
        slow_start(n, source)
        for far in range(2):
            to_fast(n, source, far).start()

    def peer(k):
        if members & (members - 1):
            return lax.rem(me_m + k, members)
        result, bit = 0, 1
        while bit < members:
            mine = lax.rem(me_m // bit, 2)
            result = result + bit * (1 - mine if k & bit else mine)
            bit *= 2
        return result

    peers = sorted(range(1, members), key=lambda k: -bin(k).count("1"))

    def to_member(step, k, i):
        return pltpu.make_async_remote_copy(
            src_ref=fields.at[step, i], dst_ref=others.at[step, k - 1, i],
            send_sem=other_send.at[step, k - 1, i], recv_sem=other_recv.at[step, k - 1, i],
            device_id={"member": peer(k)}, device_id_type=MESH)

    for fetch in fetches[:rows]:
        fetch.wait()
    pl.semaphore_wait(barrier, members + bands - 2)
    halo_start(0, x_ref)

    def put_wide(target, a, block):
        tall[0:taps, :] = block
        high, low = split(tall[...].T)
        target[a, 0:hidden] = high
        target[a, hidden:2 * hidden] = low

    def tap_rows(a):
        return pl.ds(pl.multiple_of(mirrored(a, 2) * taps, 8), taps)

    def tap_block(a, b, size, unit):
        return pl.ds(pl.multiple_of((3 * mirrored(a, 2) + b) * size, unit), size)

    def front_weights():
        fetches[rows].wait()
        fetches[rows + 2].wait()
        tall[taps:, :] = jnp.zeros((depth - taps, hidden), F32)
        for a in range(3):
            put_wide(win, a, w_in_ref[tap_rows(a), :])
        bias[...] = jnp.broadcast_to(bias_ref[...], (cols, hidden)).T
        for t in range(rows + 4):
            s_high[t * depth + taps:(t + 1) * depth, :] = jnp.zeros((depth - taps, cols), BF16)
            s_low[t * depth + taps:(t + 1) * depth, :] = jnp.zeros((depth - taps, cols), BF16)

    def narrow_weights():
        fetches[rows + 1].wait()
        for a in range(3):
            for b in range(3):
                high, low = split(w_out_ref[:, tap_block(a, b, hidden, 128)])
                wout[b * chans:(b + 1) * chans, a * hidden:(a + 1) * hidden] = high
                wout[taps + b * chans:taps + (b + 1) * chans, a * hidden:(a + 1) * hidden] = low

    def back_weights():
        for a in range(3):
            for b in range(3):
                high, low = split(w_in_ref[tap_block(2 - a, 2 - b, chans, 8), :])
                winb[b * chans:(b + 1) * chans, a * hidden:(a + 1) * hidden] = high
                winb[taps + b * chans:taps + (b + 1) * chans, a * hidden:(a + 1) * hidden] = low
        for a in range(3):
            put_wide(woutb, a, jnp.concatenate(
                [w_out_ref[:, tap_block(2 - a, 2 - b, hidden, 128)] for b in range(3)], axis=0))

    def put_line(t, line):
        for b in range(3):
            high, low = split(shifted(line, b))
            at = t * depth + b * chans
            s_high[at:at + chans, :] = high
            s_low[at:at + chans, :] = low

    def joined(ref, size, lines):
        return jnp.concatenate([ref[t * size:(t + 1) * size, :] for t in lines], axis=1)

    def widen(weights, parts):
        sums = {}
        for a, lines in parts:
            high = joined(s_high, depth, lines)
            low = joined(s_low, depth, lines)
            both = dot(weights[a], high)
            total = both[0:hidden] + both[hidden:2 * hidden] + dot(weights[a, 0:hidden, :], low)
            for n, t in enumerate(lines):
                line = total[:, n * cols:(n + 1) * cols]
                sums[t - a] = line if t - a not in sums else sums[t - a] + line
        return sums

    def narrow(weights, parts):
        sums = {}
        for a, outs in parts:
            lines = [i + a for i in outs]
            at = a * hidden
            both = dot(weights[:, at:at + hidden], joined(h_high, hidden, lines))
            total = both[0:taps] + both[taps:2 * taps] + dot(
                weights[0:taps, at:at + hidden], joined(h_low, hidden, lines))
            for n, i in enumerate(outs):
                line = total[:, n * cols:(n + 1) * cols]
                sums[i] = line if i not in sums else sums[i] + line
        return sums

    def put_hidden(j, value):
        if j == 0:
            value = jnp.where(has_slow, value, 0.0)
        high, low = split(value)
        h_high[j * hidden:(j + 1) * hidden, :] = high
        h_low[j * hidden:(j + 1) * hidden, :] = low

    def bend(step, j, value):
        value = value + bias[...]
        inner = jnp.tanh(gelu_scale * (value + gelu_cubic * value * value * value))
        put_hidden(j, 0.5 * value * (1.0 + inner))
        slope[step, j] = 0.5 * (1.0 + inner) + 0.5 * value * (1.0 - inner * inner) * (
            gelu_scale * (1.0 + 3.0 * gelu_cubic * value * value))

    def unbend(step, j, value):
        put_hidden(j, value * slope[step, j])

    def own_part(weights, own):
        for i in range(rows):
            put_line(i + 2, own[i])
        for j, line in widen(weights, [(a, range(2, rows + 2)) for a in range(3)]).items():
            before[j] = line

    def convolve(wide, slim, n, own, act):
        for far in range(2):
            to_fast(n, own, far).wait_recv()
            put_line(rows + 2 + far, halo[n, 1, far])
        sums = widen(wide, [(2, (rows + 2, rows + 3)), (1, (rows + 2,))])
        for j in range(2, rows + 2):
            act(j, before[j] + sums[j] if j in sums else before[j])
        early = [(a, [i for i in range(rows) if i + a >= 2]) for a in (2, 1, 0)]
        for i, line in narrow(slim, [part for part in early if part[1]]).items():
            narrowed[i] = line
        slow_wait(n, own, 0)
        put_line(1, halo[n, 0, 0])
        sums = widen(wide, [(0, (1,)), (1, (1,))])
        before[0] += sums[0]
        act(1, before[1] + sums[1])
        slow_wait(n, own, 1)
        put_line(0, halo[n, 0, 1])
        act(0, before[0] + widen(wide, [(0, (0,))])[0])
        sums = narrow(slim, [(1, (0,)), (0, (0, 1))])
        result = []
        for i in range(rows):
            line = narrowed[i] + sums[i] if i in sums else narrowed[i]
            result.append(sum(shifted(line[b * chans:(b + 1) * chans], b) for b in range(3)))
        return result

    def fold(value):
        return sum(value[8 * i:8 * i + 8] for i in range(chans // 8))

    def loss_terms(step, i):
        weight = jnp.where(odd == 1, lat_ref[0:1, rows - 1 - i:rows - i], lat_ref[0:1, i:i + 1])
        mine = fields[step, i]
        error = mine - target_ref[step, i]
        square = error * error + smooth_width * smooth_width
        inverse = lax.rsqrt(square)
        direct = square * inverse
        gradient = error * inverse
        summed = jnp.full(mine.shape, smooth_width, F32)
        slopes = jnp.zeros_like(mine)
        for k in range(1, members):
            spread = mine - others[step, k - 1, i]
            square = spread * spread + smooth_width * smooth_width
            inverse = lax.rsqrt(square)
            summed = summed + square * inverse
            slopes = slopes + spread * inverse
        loss_grad[step, i] = weight * (gradient - slopes / (members - 1))
        return weight * fold(direct - summed / (2.0 * (members - 1)))

    for step in range(steps):
        own = x_ref if step == 0 else fields.at[step - 1]
        if step == 0:
            front_weights()
        own_part(win, own)
        if step == 0:
            narrow_weights()
        else:
            back_weights()
        change = convolve(win, wout, step, own, functools.partial(bend, step))
        for i in range(rows):
            fields[step, i] = own[i] + change[i]
        if step < steps - 1:
            halo_start(step + 1, fields.at[step])
        for i in range(rows):
            for k in peers:
                to_member(step, k, i).start()

    for fetch in fetches[rows + 3:]:
        fetch.wait()
    partial = jnp.zeros((8, cols), F32)
    for step in range(steps):
        for i in range(rows):
            for k in peers:
                to_member(step, k, i).wait()
            partial = partial + loss_terms(step, i)
            if step == steps - 1:
                grads[step, i] = loss_grad[step, i]
                if i < 2:
                    slow_start(steps, grads.at[step], (i,))
                if rows - 1 - i < 2:
                    to_fast(steps, grads.at[step], rows - 1 - i).start()

    def part_to_member(k):
        return pltpu.make_async_remote_copy(
            src_ref=part_src.at[0], dst_ref=parts_m.at[me_m],
            send_sem=pm_send.at[k - 1], recv_sem=pm_recv.at[me_m],
            device_id={"member": lax.rem(me_m + k, members)}, device_id_type=MESH)

    def part_from_member(k):
        source = lax.rem(me_m + k, members)
        return pltpu.make_async_remote_copy(
            src_ref=part_src.at[0], dst_ref=parts_m.at[source],
            send_sem=pm_send.at[k - 1], recv_sem=pm_recv.at[source],
            device_id={"member": source}, device_id_type=MESH)

    def part_to_band(k):
        return pltpu.make_async_remote_copy(
            src_ref=part_src.at[1], dst_ref=parts_l.at[me_l],
            send_sem=pl_send.at[k - 1], recv_sem=pl_recv.at[me_l],
            device_id={"lat": lax.rem(me_l + k, bands)}, device_id_type=MESH)

    def part_from_band(k):
        source = lax.rem(me_l + k, bands)
        return pltpu.make_async_remote_copy(
            src_ref=part_src.at[1], dst_ref=parts_l.at[source],
            send_sem=pl_send.at[k - 1], recv_sem=pl_recv.at[source],
            device_id={"lat": source}, device_id_type=MESH)

    part_src[0] = partial

    for step in range(steps - 1, -1, -1):
        n = 2 * steps - 1 - step
        own = grads.at[step]
        if step == steps - 1:
            for k in range(1, members):
                part_to_member(k).start()
            parts_m[me_m] = partial
        else:
            for i in range(rows):
                grads[step, i] = grads[step + 1, i] + change[i] + loss_grad[step, i]
            halo_start(n, own)
            if step == steps - 2:
                for k in range(1, members):
                    part_to_member(k).wait_send()
                    part_from_member(k).wait_recv()
                total = sum(parts_m[k] for k in range(members))
                part_src[1] = total
                for k in range(1, bands):
                    part_to_band(k).start()
                parts_l[me_l] = total
        own_part(woutb, own)
        change = convolve(woutb, winb, n, own, functools.partial(unbend, step))

    for i in range(rows):
        grad_ref[mirrored(i, rows - 1)] = grads[0, i] + change[i]
    for k in range(1, bands):
        part_to_band(k).wait_send()
        part_from_band(k).wait_recv()
    total = sum(parts_l[k] for k in range(bands))
    count = members * steps * rows * bands * chans * cols
    loss_ref[...] = jnp.full(loss_ref.shape, jnp.sum(total) / count, F32)
    for n in range(2 * steps):
        own = x_ref if n == 0 else fields.at[n - 1] if n < steps else grads.at[2 * steps - 1 - n]
        for far in range(2):
            to_fast(n, own, far).wait_send()

        @pl.when(has_slow)
        def _():
            for far in range(2):
                to_slow(n, own, far).wait_send()


def deliver(grad_vmem, loss_vmem, grad_hbm, loss_hbm, loss_smem, sem):
    gradient = pltpu.make_async_copy(grad_vmem, grad_hbm, sem.at[0])
    loss = pltpu.make_async_copy(loss_smem, loss_hbm, sem.at[1])
    gradient.start()
    loss_smem[0, 0] = loss_vmem[0, 0]
    loss.start()
    loss.wait()
    gradient.wait()


def on_device(members, bands, initial_states, targets, lat_weight, weight_in, weight_out, hidden_bias):
    steps, rows, chans, cols = targets.shape
    hidden = weight_in.shape[0]
    taps = 3 * chans
    depth = -(-taps // 256) * 256
    deep = 3 * hidden
    vmem = pl.BlockSpec(memory_space=pltpu.VMEM)
    dma = pltpu.SemaphoreType.DMA
    gradient, loss = pl.pallas_call(
        functools.partial(kernel, members, bands),
        out_shape=(pltpu.VMEM((rows, chans, cols), F32), pltpu.VMEM((8, cols), F32)),
        in_specs=[pl.BlockSpec(memory_space=pltpu.HBM)] * 6,
        out_specs=(vmem, vmem),
        scratch_shapes=[
            pltpu.VMEM((rows, chans, cols), F32),
            pltpu.VMEM(targets.shape, F32),
            pltpu.VMEM((1, rows), F32),
            pltpu.VMEM((3 * taps, hidden), F32),
            pltpu.VMEM((chans, 3 * deep), F32),
            pltpu.VMEM((1, hidden), F32),
            dma((2 * rows + 4,)),
            pltpu.VMEM((2 * steps, 2, 2, chans, cols), F32),
            pltpu.VMEM((steps, members - 1, rows, chans, cols), F32),
            pltpu.VMEM((members, 8, cols), F32),
            pltpu.VMEM((bands, 8, cols), F32),
            pltpu.VMEM((steps, rows, chans, cols), F32),
            pltpu.VMEM((steps, rows, chans, cols), F32),
            pltpu.VMEM((2, 8, cols), F32),
            pltpu.VMEM((3, 2 * hidden, depth), BF16),
            pltpu.VMEM((2 * taps, deep), BF16),
            pltpu.VMEM((2 * taps, deep), BF16),
            pltpu.VMEM((3, 2 * hidden, depth), BF16),
            pltpu.VMEM((depth, hidden), F32),
            pltpu.VMEM(((rows + 4) * depth, cols), BF16),
            pltpu.VMEM(((rows + 4) * depth, cols), BF16),
            pltpu.VMEM(((rows + 2) * hidden, cols), BF16),
            pltpu.VMEM(((rows + 2) * hidden, cols), BF16),
            pltpu.VMEM((rows + 2, hidden, cols), F32),
            pltpu.VMEM((steps, rows + 2, hidden, cols), F32),
            pltpu.VMEM((rows, taps, cols), F32),
            pltpu.VMEM((steps, rows, chans, cols), F32),
            pltpu.VMEM((hidden, cols), F32),
            dma((2 * steps, 2, 2)), dma((2 * steps, 2, 2)),
            dma((steps, members - 1, rows)), dma((steps, members - 1, rows)),
            dma((members - 1,)), dma((members,)),
            dma((bands - 1,)), dma((bands,)),
        ],
        compiler_params=pltpu.CompilerParams(collective_id=0, has_side_effects=True, vmem_limit_bytes=24 * 2**20),
    )(
        *(pltpu.with_memory_space_constraint(value, pltpu.HBM) for value in (
            initial_states.reshape(rows, chans, cols), targets, lat_weight.reshape(1, rows),
            weight_in.T, weight_out, hidden_bias.reshape(1, hidden)))
    )
    anywhere = pl.BlockSpec(memory_space=pl.ANY)
    gradient, loss = pl.pallas_call(
        deliver,
        out_shape=(jax.ShapeDtypeStruct((rows, chans, cols), F32), jax.ShapeDtypeStruct((1, 1), F32)),
        in_specs=[vmem, vmem],
        out_specs=(anywhere, anywhere),
        scratch_shapes=[pltpu.SMEM((1, 1), F32), dma((2,))],
    )(*(pltpu.with_memory_space_constraint(value, pltpu.VMEM) for value in (gradient, loss)))
    return gradient.reshape(initial_states.shape), loss.reshape(())


def solution(mesh):
    placed = (P("member", "lat", None, None), P(None, "lat", None, None), P("lat"), P(), P(), P())
    return jax.shard_map(
        functools.partial(on_device, mesh.shape["member"], mesh.shape["lat"]),
        mesh=mesh,
        in_specs=placed,
        out_specs=(P("member", "lat", None, None), P()),
        check_vma=False,
    )
```

time: 30.2 us -> 28.7 us (0.950)
  Pallas kernels: 29.3 us -> 28 us
    pallas_call x1, Pallas kernels: 28.6 us -> 27.3 us  [on_device(): pl.pallas_call(functools.partial(kernel, members, bands), out_shape=(pltp...]
where the time goes in v2:
time: 28.7 us; the launch traced here: 28.6 us
  Pallas kernels  28 us (98%)
  between operations  0.64 us (2%)
    pallas_call x1, Pallas kernels, on_device(): pl.pallas_call(functools.partial(kernel, members, bands), out_shape=(pltp...  27.3 us
    pallas_call x1, Pallas kernels, on_device(): pl.pallas_call(deliver, out_shape=(jax.ShapeDtypeStruct((rows, chans, col...  0.66 us

profile of v2, /device:TPU:1, one launch (start us, length us, event | category | flops | bytes accessed | tf_op | source)
XLA Modules:
  0.0 28.6 jit_solution(10037013210207079739)
XLA Ops:
  0.6 27.3 %shard_map.77 = (f32[2,80,128]{2,1,0:T(8,128)S(1)}, f32[8,128]{1,0:T(8,128)S(1)}) custom-call(f32[2,80,128]{2,1,0:T(8,128)} %bitcast.7, f32[2,2,80,128]{3,2,1,0:T(8,128)} %target_hbm.1, f32[1,2]{1,0:T(1,128)} %bitcast.9, f32[720,256]{1,0:T(8,128)} %bitcast.6, f32[80,2304]{1,0:T(8,128)} %w_out_hbm.1, f32[1,256]{1,0:T(1,128)} %bitcast.8), custom_call_target="tpu_custom_call" | custom-call | tf_op jit(solution)/shard_map/pallas_call | solution.py:401
  27.9 0.7 %shard_map.78 = (f32[2,80,128]{2,1,0:T(8,128)}, f32[1,1]{1,0:T(1,128)}) custom-call(f32[2,80,128]{2,1,0:T(8,128)S(1)} %get-tuple-element.6.grad_vmem, f32[8,128]{1,0:T(8,128)S(1)} %get-tuple-element.7.loss_vmem), custom_call_target="tpu_custom_call" | custom-call | tf_op jit(solution)/shard_map/pallas_call | solution.py:447

commit v3 on v2

--- a/solution.py
+++ b/solution.py
@@ -40,9 +40,9 @@
     x_hbm, target_hbm, lat_hbm, w_in_hbm, w_out_hbm, bias_hbm,
     grad_ref, loss_ref,
     x_ref, target_ref, lat_ref, w_in_ref, w_out_ref, bias_ref, fetch_sem,
-    halo, others, parts_m, parts_l, fields, grads, part_src,
+    halo, others, parts, fields, grads,
     win, winb, wout, woutb, tall, s_high, s_low, h_high, h_low, before, slope, narrowed, loss_grad, bias,
-    halo_send, halo_recv, other_send, other_recv, pm_send, pm_recv, pl_send, pl_recv,
+    halo_send, slow_recv, fast_recv, other_send, other_recv, part_send, part_recv, reach,
 ):
     steps, rows, chans, cols = target_ref.shape
     hidden = w_in_ref.shape[1]
@@ -59,21 +59,37 @@
     def mirrored(n, last):
         return n + odd * (last - 2 * n)
 
+    def fetch(n, copies):
+        return [pltpu.make_async_copy(source, target, fetch_sem.at[n]) for source, target in copies]
+
+    mirror = [mirrored(i, rows - 1) for i in range(rows)]
     fetches = [
-        pltpu.make_async_copy(source, target, fetch_sem.at[n])
-        for n, (source, target) in enumerate(
-            [(x_hbm.at[mirrored(i, rows - 1)], x_ref.at[i]) for i in range(rows)]
-            + [(w_in_hbm, w_in_ref), (w_out_hbm, w_out_ref), (bias_hbm, bias_ref), (lat_hbm, lat_ref)]
-            + [(target_hbm.at[:, mirrored(i, rows - 1)], target_ref.at[:, i]) for i in range(rows)])
+        fetch(0, [(x_hbm.at[mirror[i]], x_ref.at[i]) for i in range(rows)]),
+        fetch(1, [(w_in_hbm, w_in_ref)]),
+        fetch(2, [(bias_hbm, bias_ref)]),
+        fetch(3, [(w_out_hbm, w_out_ref)]),
+        fetch(4, [(target_hbm.at[:, mirror[i]], target_ref.at[:, i]) for i in range(rows)]),
+        fetch(5, [(lat_hbm, lat_ref)]),
     ]
+    arrivals = [x_ref, w_in_ref, bias_ref, w_out_ref, target_ref, lat_ref]
+
+    def arrive(n):
+        pltpu.make_async_copy(arrivals[n], arrivals[n], fetch_sem.at[n]).wait()
+
+    for copy in fetches[0]:
+        copy.start()
     barrier = pltpu.get_barrier_semaphore()
     for k in range(1, members):
         pl.semaphore_signal(barrier, inc=1, device_id={"member": lax.rem(me_m + k, members)}, device_id_type=MESH)
-    for k in range(1, bands):
-        pl.semaphore_signal(barrier, inc=1, device_id={"lat": lax.rem(me_l + k, bands)}, device_id_type=MESH)
-
-    for fetch in fetches:
-        fetch.start()
+    pl.semaphore_signal(barrier, inc=1, device_id={"lat": fast}, device_id_type=MESH)
+
+    @pl.when(has_slow)
+    def _():
+        pl.semaphore_signal(barrier, inc=1, device_id={"lat": slow}, device_id_type=MESH)
+
+    for copies in fetches[1:]:
+        for copy in copies:
+            copy.start()
 
     @pl.when(jnp.logical_not(has_slow))
     def _():
@@ -83,13 +99,13 @@
     def to_slow(n, source, far):
         return pltpu.make_async_remote_copy(
             src_ref=source.at[far], dst_ref=halo.at[n, 0, far],
-            send_sem=halo_send.at[n, 0, far], recv_sem=halo_recv.at[n, 0, far],
+            send_sem=halo_send.at[0], recv_sem=slow_recv.at[n, far],
             device_id={"lat": slow}, device_id_type=MESH)
 
     def to_fast(n, source, far):
         return pltpu.make_async_remote_copy(
             src_ref=source.at[rows - 1 - far], dst_ref=halo.at[n, 1, far],
-            send_sem=halo_send.at[n, 1, far], recv_sem=halo_recv.at[n, 1, far],
+            send_sem=halo_send.at[1], recv_sem=fast_recv.at[n],
             device_id={"lat": fast}, device_id_type=MESH)
 
     def slow_start(n, source, fars=(0, 1)):
@@ -123,13 +139,29 @@
     def to_member(step, k, i):
         return pltpu.make_async_remote_copy(
             src_ref=fields.at[step, i], dst_ref=others.at[step, k - 1, i],
-            send_sem=other_send.at[step, k - 1, i], recv_sem=other_recv.at[step, k - 1, i],
+            send_sem=other_send.at[0], recv_sem=other_recv.at[step, i],
             device_id={"member": peer(k)}, device_id_type=MESH)
 
-    for fetch in fetches[:rows]:
-        fetch.wait()
-    pl.semaphore_wait(barrier, members + bands - 2)
+    rounds = [1]
+    while 2 * rounds[-1] < bands - 1:
+        rounds.append(2 * rounds[-1])
+
+    def reach_out(r):
+        for far in (me_l - rounds[r], me_l + rounds[r]):
+            @pl.when(jnp.logical_and(far >= 0, far < bands))
+            def _():
+                pl.semaphore_signal(
+                    reach.at[r], inc=1, device_id={"lat": jnp.clip(far, 0, bands - 1)}, device_id_type=MESH)
+
+    def reached(r):
+        below = (me_l >= rounds[r]).astype(jnp.int32)
+        above = (me_l + rounds[r] < bands).astype(jnp.int32)
+        pl.semaphore_wait(reach.at[r], below + above)
+
+    arrive(0)
+    pl.semaphore_wait(barrier, members + has_slow.astype(jnp.int32))
     halo_start(0, x_ref)
+    reach_out(0)
 
     def put_wide(target, a, block):
         tall[0:taps, :] = block
@@ -144,8 +176,8 @@
         return pl.ds(pl.multiple_of((3 * mirrored(a, 2) + b) * size, unit), size)
 
     def front_weights():
-        fetches[rows].wait()
-        fetches[rows + 2].wait()
+        arrive(1)
+        arrive(2)
         tall[taps:, :] = jnp.zeros((depth - taps, hidden), F32)
         for a in range(3):
             put_wide(win, a, w_in_ref[tap_rows(a), :])
@@ -155,7 +187,7 @@
             s_low[t * depth + taps:(t + 1) * depth, :] = jnp.zeros((depth - taps, cols), BF16)
 
     def narrow_weights():
-        fetches[rows + 1].wait()
+        arrive(3)
         for a in range(3):
             for b in range(3):
                 high, low = split(w_out_ref[:, tap_block(a, b, hidden, 128)])
@@ -231,8 +263,8 @@
             before[j] = line
 
     def convolve(wide, slim, n, own, act):
+        pltpu.make_async_copy(halo.at[n, 1], halo.at[n, 1], fast_recv.at[n]).wait()
         for far in range(2):
-            to_fast(n, own, far).wait_recv()
             put_line(rows + 2 + far, halo[n, 1, far])
         sums = widen(wide, [(2, (rows + 2, rows + 3)), (1, (rows + 2,))])
         for j in range(2, rows + 2):
@@ -286,22 +318,31 @@
             narrow_weights()
         else:
             back_weights()
+        if step < len(rounds):
+            reached(step)
+            if step + 1 < len(rounds):
+                reach_out(step + 1)
         change = convolve(win, wout, step, own, functools.partial(bend, step))
         for i in range(rows):
             fields[step, i] = own[i] + change[i]
         if step < steps - 1:
             halo_start(step + 1, fields.at[step])
+        if step == steps - 1:
+            for r in range(steps, len(rounds)):
+                reached(r)
+                if r + 1 < len(rounds):
+                    reach_out(r + 1)
         for i in range(rows):
             for k in peers:
                 to_member(step, k, i).start()
 
-    for fetch in fetches[rows + 3:]:
-        fetch.wait()
+    arrive(4)
+    arrive(5)
     partial = jnp.zeros((8, cols), F32)
     for step in range(steps):
         for i in range(rows):
-            for k in peers:
-                to_member(step, k, i).wait()
+            landed = others.at[step, :, i]
+            pltpu.make_async_copy(landed, landed, other_recv.at[step, i]).wait()
             partial = partial + loss_terms(step, i)
             if step == steps - 1:
                 grads[step, i] = loss_grad[step, i]
@@ -310,74 +351,38 @@
                 if rows - 1 - i < 2:
                     to_fast(steps, grads.at[step], rows - 1 - i).start()
 
-    def part_to_member(k):
-        return pltpu.make_async_remote_copy(
-            src_ref=part_src.at[0], dst_ref=parts_m.at[me_m],
-            send_sem=pm_send.at[k - 1], recv_sem=pm_recv.at[me_m],
-            device_id={"member": lax.rem(me_m + k, members)}, device_id_type=MESH)
-
-    def part_from_member(k):
-        source = lax.rem(me_m + k, members)
-        return pltpu.make_async_remote_copy(
-            src_ref=part_src.at[0], dst_ref=parts_m.at[source],
-            send_sem=pm_send.at[k - 1], recv_sem=pm_recv.at[source],
-            device_id={"member": source}, device_id_type=MESH)
-
-    def part_to_band(k):
-        return pltpu.make_async_remote_copy(
-            src_ref=part_src.at[1], dst_ref=parts_l.at[me_l],
-            send_sem=pl_send.at[k - 1], recv_sem=pl_recv.at[me_l],
-            device_id={"lat": lax.rem(me_l + k, bands)}, device_id_type=MESH)
-
-    def part_from_band(k):
-        source = lax.rem(me_l + k, bands)
-        return pltpu.make_async_remote_copy(
-            src_ref=part_src.at[1], dst_ref=parts_l.at[source],
-            send_sem=pl_send.at[k - 1], recv_sem=pl_recv.at[source],
-            device_id={"lat": source}, device_id_type=MESH)
-
-    part_src[0] = partial
+    me = me_m * bands + me_l
+    parts[me] = jnp.sum(partial, axis=0, keepdims=True)
+    for n in range(1, members * bands):
+        pltpu.make_async_remote_copy(
+            src_ref=parts.at[me], dst_ref=parts.at[me], send_sem=part_send.at[0], recv_sem=part_recv.at[0],
+            device_id={"member": lax.rem(me_m + n // bands, members), "lat": lax.rem(me_l + n % bands, bands)},
+            device_id_type=MESH).start()
 
     for step in range(steps - 1, -1, -1):
         n = 2 * steps - 1 - step
         own = grads.at[step]
-        if step == steps - 1:
-            for k in range(1, members):
-                part_to_member(k).start()
-            parts_m[me_m] = partial
-        else:
+        if step < steps - 1:
             for i in range(rows):
                 grads[step, i] = grads[step + 1, i] + change[i] + loss_grad[step, i]
             halo_start(n, own)
-            if step == steps - 2:
-                for k in range(1, members):
-                    part_to_member(k).wait_send()
-                    part_from_member(k).wait_recv()
-                total = sum(parts_m[k] for k in range(members))
-                part_src[1] = total
-                for k in range(1, bands):
-                    part_to_band(k).start()
-                parts_l[me_l] = total
         own_part(woutb, own)
         change = convolve(woutb, winb, n, own, functools.partial(unbend, step))
 
     for i in range(rows):
         grad_ref[mirrored(i, rows - 1)] = grads[0, i] + change[i]
-    for k in range(1, bands):
-        part_to_band(k).wait_send()
-        part_from_band(k).wait_recv()
-    total = sum(parts_l[k] for k in range(bands))
+    sent = parts.at[0:members * bands - 1]
+    pltpu.make_async_copy(sent, sent, part_recv.at[0]).wait()
+    total = jnp.sum(parts[...], axis=0)
     count = members * steps * rows * bands * chans * cols
     loss_ref[...] = jnp.full(loss_ref.shape, jnp.sum(total) / count, F32)
-    for n in range(2 * steps):
-        own = x_ref if n == 0 else fields.at[n - 1] if n < steps else grads.at[2 * steps - 1 - n]
-        for far in range(2):
-            to_fast(n, own, far).wait_send()
-
-        @pl.when(has_slow)
-        def _():
-            for far in range(2):
-                to_slow(n, own, far).wait_send()
+    pltpu.make_async_copy(sent, sent, part_send.at[0]).wait()
+    pltpu.make_async_copy(others, others, other_send.at[0]).wait()
+    pltpu.make_async_copy(halo.at[:, 1], halo.at[:, 1], halo_send.at[1]).wait()
+
+    @pl.when(has_slow)
+    def _():
+        pltpu.make_async_copy(halo.at[:, 0], halo.at[:, 0], halo_send.at[0]).wait()
 
 
 def deliver(grad_vmem, loss_vmem, grad_hbm, loss_hbm, loss_smem, sem):
@@ -410,14 +415,12 @@
             pltpu.VMEM((3 * taps, hidden), F32),
             pltpu.VMEM((chans, 3 * deep), F32),
             pltpu.VMEM((1, hidden), F32),
-            dma((2 * rows + 4,)),
+            dma((6,)),
             pltpu.VMEM((2 * steps, 2, 2, chans, cols), F32),
             pltpu.VMEM((steps, members - 1, rows, chans, cols), F32),
-            pltpu.VMEM((members, 8, cols), F32),
-            pltpu.VMEM((bands, 8, cols), F32),
+            pltpu.VMEM((members * bands, 1, cols), F32),
             pltpu.VMEM((steps, rows, chans, cols), F32),
             pltpu.VMEM((steps, rows, chans, cols), F32),
-            pltpu.VMEM((2, 8, cols), F32),
             pltpu.VMEM((3, 2 * hidden, depth), BF16),
             pltpu.VMEM((2 * taps, deep), BF16),
             pltpu.VMEM((2 * taps, deep), BF16),
@@ -432,10 +435,10 @@
             pltpu.VMEM((rows, taps, cols), F32),
             pltpu.VMEM((steps, rows, chans, cols), F32),
             pltpu.VMEM((hidden, cols), F32),
-            dma((2 * steps, 2, 2)), dma((2 * steps, 2, 2)),
-            dma((steps, members - 1, rows)), dma((steps, members - 1, rows)),
-            dma((members - 1,)), dma((members,)),
-            dma((bands - 1,)), dma((bands,)),
+            dma((2,)), dma((2 * steps, 2)), dma((2 * steps,)),
+            dma((1,)), dma((steps, rows)),
+            dma((1,)), dma((1,)),
+            pltpu.SemaphoreType.REGULAR((max(1, (bands - 2).bit_length()),)),
         ],
         compiler_params=pltpu.CompilerParams(collective_id=0, has_side_effects=True, vmem_limit_bytes=24 * 2**20),
     )(

time: 28.7 us -> 26.8 us (0.934); the launches traced: 28.6 us -> 26.3 us
  Pallas kernels: 28 us -> 25.7 us
    pallas_call x1, Pallas kernels: 27.3 us -> 25.1 us  [on_device(): pl.pallas_call(functools.partial(kernel, members, bands), out_shape=(pltp...]
where the time goes in v3:
time: 26.8 us; the launch traced here: 26.3 us
  Pallas kernels  25.7 us (96%)
  between operations  0.64 us (2%)
    pallas_call x1, Pallas kernels, on_device(): pl.pallas_call(functools.partial(kernel, members, bands), out_shape=(pltp...  25.1 us
    pallas_call x1, Pallas kernels, on_device(): pl.pallas_call(deliver, out_shape=(jax.ShapeDtypeStruct((rows, chans, col...  0.66 us

profile of v3, /device:TPU:1, one launch (start us, length us, event | category | flops | bytes accessed | tf_op | source)
XLA Modules:
  0.0 26.3 jit_solution(2691021649395974432)
XLA Ops:
  0.6 25.1 %shard_map.77 = (f32[2,80,128]{2,1,0:T(8,128)S(1)}, f32[8,128]{1,0:T(8,128)S(1)}) custom-call(f32[2,80,128]{2,1,0:T(8,128)} %bitcast.7, f32[2,2,80,128]{3,2,1,0:T(8,128)} %target_hbm.1, f32[1,2]{1,0:T(1,128)} %bitcast.9, f32[720,256]{1,0:T(8,128)} %bitcast.6, f32[80,2304]{1,0:T(8,128)} %w_out_hbm.1, f32[1,256]{1,0:T(1,128)} %bitcast.8), custom_call_target="tpu_custom_call" | custom-call | tf_op jit(solution)/shard_map/pallas_call | solution.py:406
  25.7 0.7 %shard_map.78 = (f32[2,80,128]{2,1,0:T(8,128)}, f32[1,1]{1,0:T(1,128)}) custom-call(f32[2,80,128]{2,1,0:T(8,128)S(1)} %get-tuple-element.6.grad_vmem, f32[8,128]{1,0:T(8,128)S(1)} %get-tuple-element.7.loss_vmem), custom_call_target="tpu_custom_call" | custom-call | tf_op jit(solution)/shard_map/pallas_call | solution.py:450

commit v4 on v3

--- a/solution.py
+++ b/solution.py
@@ -41,7 +41,7 @@
     grad_ref, loss_ref,
     x_ref, target_ref, lat_ref, w_in_ref, w_out_ref, bias_ref, fetch_sem,
     halo, others, parts, fields, grads,
-    win, winb, wout, woutb, tall, s_high, s_low, h_high, h_low, before, slope, narrowed, loss_grad, bias,
+    win, winb, wout, woutb, tall, s_high, s_low, h_high, h_low, before, slope, bent, narrowed, edge, loss_grad, bias,
     halo_send, slow_recv, fast_recv, other_send, other_recv, part_send, part_recv, reach,
 ):
     steps, rows, chans, cols = target_ref.shape
@@ -91,11 +91,6 @@
         for copy in copies:
             copy.start()
 
-    @pl.when(jnp.logical_not(has_slow))
-    def _():
-        for n in range(2 * steps):
-            halo[n, 0] = jnp.zeros(halo.shape[2:], F32)
-
     def to_slow(n, source, far):
         return pltpu.make_async_remote_copy(
             src_ref=source.at[far], dst_ref=halo.at[n, 0, far],
@@ -108,21 +103,14 @@
             send_sem=halo_send.at[1], recv_sem=fast_recv.at[n],
             device_id={"lat": fast}, device_id_type=MESH)
 
-    def slow_start(n, source, fars=(0, 1)):
-        @pl.when(has_slow)
-        def _():
-            for far in fars:
-                to_slow(n, source, far).start()
-
-    def slow_wait(n, source, far):
-        @pl.when(has_slow)
-        def _():
-            to_slow(n, source, far).wait_recv()
-
-    def halo_start(n, source):
-        slow_start(n, source)
-        for far in range(2):
-            to_fast(n, source, far).start()
+    def send_row(n, source, i):
+        if i < 2:
+            @pl.when(has_slow)
+            def _():
+                to_slow(n, source, i).start()
+
+        if rows - 1 - i < 2:
+            to_fast(n, source, rows - 1 - i).start()
 
     def peer(k):
         if members & (members - 1):
@@ -160,7 +148,8 @@
 
     arrive(0)
     pl.semaphore_wait(barrier, members + has_slow.astype(jnp.int32))
-    halo_start(0, x_ref)
+    for i in range(rows):
+        send_row(0, x_ref, i)
     reach_out(0)
 
     def put_wide(target, a, block):
@@ -191,15 +180,15 @@
         for a in range(3):
             for b in range(3):
                 high, low = split(w_out_ref[:, tap_block(a, b, hidden, 128)])
-                wout[b * chans:(b + 1) * chans, a * hidden:(a + 1) * hidden] = high
-                wout[taps + b * chans:taps + (b + 1) * chans, a * hidden:(a + 1) * hidden] = low
+                wout[a, b * chans:(b + 1) * chans, :] = high
+                wout[a, taps + b * chans:taps + (b + 1) * chans, :] = low
 
     def back_weights():
         for a in range(3):
             for b in range(3):
                 high, low = split(w_in_ref[tap_block(2 - a, 2 - b, chans, 8), :])
-                winb[b * chans:(b + 1) * chans, a * hidden:(a + 1) * hidden] = high
-                winb[taps + b * chans:taps + (b + 1) * chans, a * hidden:(a + 1) * hidden] = low
+                winb[a, b * chans:(b + 1) * chans, :] = high
+                winb[a, taps + b * chans:taps + (b + 1) * chans, :] = low
         for a in range(3):
             put_wide(woutb, a, jnp.concatenate(
                 [w_out_ref[:, tap_block(2 - a, 2 - b, hidden, 128)] for b in range(3)], axis=0))
@@ -226,22 +215,39 @@
                 sums[t - a] = line if t - a not in sums else sums[t - a] + line
         return sums
 
+    def half(weights, a, high, low):
+        both = jnp.concatenate([high, low], axis=1)
+        size = weights.shape[1] // 2
+        middle = -(-size // 32) * 16
+        lines = []
+        for first, last in ((0, middle), (middle, size)):
+            line = dot(weights[a, first:last, :], both) + dot(weights[a, size + first:size + last, :], both)
+            lines.append(line[:, 0:cols] + line[:, cols:2 * cols])
+        return jnp.concatenate(lines, axis=0)
+
+    def widen_line(weights, a, t):
+        at = t * depth
+        return half(weights, a, s_high[at:at + depth, :], s_low[at:at + depth, :])
+
+    def narrow_line(weights, a, j):
+        at = j * hidden
+        return half(weights, a, h_high[at:at + hidden, :], h_low[at:at + hidden, :])
+
+    def collect(total):
+        return sum(shifted(total[b * chans:(b + 1) * chans], b) for b in range(3))
+
     def narrow(weights, parts):
         sums = {}
         for a, outs in parts:
             lines = [i + a for i in outs]
-            at = a * hidden
-            both = dot(weights[:, at:at + hidden], joined(h_high, hidden, lines))
-            total = both[0:taps] + both[taps:2 * taps] + dot(
-                weights[0:taps, at:at + hidden], joined(h_low, hidden, lines))
+            both = dot(weights[a], joined(h_high, hidden, lines))
+            total = both[0:taps] + both[taps:2 * taps] + dot(weights[a, 0:taps, :], joined(h_low, hidden, lines))
             for n, i in enumerate(outs):
                 line = total[:, n * cols:(n + 1) * cols]
                 sums[i] = line if i not in sums else sums[i] + line
         return sums
 
     def put_hidden(j, value):
-        if j == 0:
-            value = jnp.where(has_slow, value, 0.0)
         high, low = split(value)
         h_high[j * hidden:(j + 1) * hidden, :] = high
         h_low[j * hidden:(j + 1) * hidden, :] = low
@@ -250,42 +256,61 @@
         value = value + bias[...]
         inner = jnp.tanh(gelu_scale * (value + gelu_cubic * value * value * value))
         put_hidden(j, 0.5 * value * (1.0 + inner))
-        slope[step, j] = 0.5 * (1.0 + inner) + 0.5 * value * (1.0 - inner * inner) * (
-            gelu_scale * (1.0 + 3.0 * gelu_cubic * value * value))
+        slope[step, j] = value
+        bent[step, j] = inner
+
+    def slopes_of(step):
+        for j in range(rows + 2):
+            value, inner = slope[step, j], bent[step, j]
+            slope[step, j] = 0.5 * (1.0 + inner) + 0.5 * value * (1.0 - inner * inner) * (
+                gelu_scale * (1.0 + 3.0 * gelu_cubic * value * value))
 
     def unbend(step, j, value):
         put_hidden(j, value * slope[step, j])
 
-    def own_part(weights, own):
+    def own_part(wide, slim, own, act):
         for i in range(rows):
             put_line(i + 2, own[i])
-        for j, line in widen(weights, [(a, range(2, rows + 2)) for a in range(3)]).items():
+        for j, line in widen(wide, [(a, range(2, rows + 2)) for a in range(3)]).items():
             before[j] = line
 
-    def convolve(wide, slim, n, own, act):
+        @pl.when(jnp.logical_not(has_slow))
+        def _():
+            act(1, before[1])
+            for i in range(2):
+                edge[i] = narrow_line(slim, 1 - i, 1)
+
+    def convolve(wide, slim, n, own, act, finish, pause=lambda: None):
         pltpu.make_async_copy(halo.at[n, 1], halo.at[n, 1], fast_recv.at[n]).wait()
         for far in range(2):
             put_line(rows + 2 + far, halo[n, 1, far])
         sums = widen(wide, [(2, (rows + 2, rows + 3)), (1, (rows + 2,))])
         for j in range(2, rows + 2):
             act(j, before[j] + sums[j] if j in sums else before[j])
-        early = [(a, [i for i in range(rows) if i + a >= 2]) for a in (2, 1, 0)]
-        for i, line in narrow(slim, [part for part in early if part[1]]).items():
-            narrowed[i] = line
-        slow_wait(n, own, 0)
-        put_line(1, halo[n, 0, 0])
-        sums = widen(wide, [(0, (1,)), (1, (1,))])
-        before[0] += sums[0]
-        act(1, before[1] + sums[1])
-        slow_wait(n, own, 1)
-        put_line(0, halo[n, 0, 1])
-        act(0, before[0] + widen(wide, [(0, (0,))])[0])
-        sums = narrow(slim, [(1, (0,)), (0, (0, 1))])
-        result = []
-        for i in range(rows):
-            line = narrowed[i] + sums[i] if i in sums else narrowed[i]
-            result.append(sum(shifted(line[b * chans:(b + 1) * chans], b) for b in range(3)))
-        return result
+        ready = [(a, [i for i in range(rows) if i + a >= 2]) for a in (2, 1, 0)]
+        for i, line in narrow(slim, [part for part in ready if part[1]]).items():
+            if i < 2:
+                narrowed[i] = line
+            else:
+                finish(i, collect(line))
+        pause()
+
+        @pl.when(jnp.logical_not(has_slow))
+        def _():
+            for i in (1, 0):
+                finish(i, collect(narrowed[i] + edge[i]))
+
+        @pl.when(has_slow)
+        def _():
+            to_slow(n, own, 1).wait_recv()
+            put_line(0, halo[n, 0, 1])
+            before[0] += widen_line(wide, 0, 0)
+            to_slow(n, own, 0).wait_recv()
+            put_line(1, halo[n, 0, 0])
+            act(1, before[1] + widen_line(wide, 0, 1))
+            act(0, before[0] + widen_line(wide, 1, 1))
+            finish(1, collect(narrowed[1] + narrow_line(slim, 0, 1)))
+            finish(0, collect(narrowed[0] + narrow_line(slim, 1, 1) + narrow_line(slim, 0, 0)))
 
     def fold(value):
         return sum(value[8 * i:8 * i + 8] for i in range(chans // 8))
@@ -313,64 +338,75 @@
         own = x_ref if step == 0 else fields.at[step - 1]
         if step == 0:
             front_weights()
-        own_part(win, own)
-        if step == 0:
             narrow_weights()
-        else:
+        act = functools.partial(bend, step)
+        own_part(win, wout, own, act)
+        if step > 0:
             back_weights()
         if step < len(rounds):
             reached(step)
             if step + 1 < len(rounds):
                 reach_out(step + 1)
-        change = convolve(win, wout, step, own, functools.partial(bend, step))
-        for i in range(rows):
-            fields[step, i] = own[i] + change[i]
+
+        def advance(i, change):
+            fields[step, i] = own[i] + change
+            if step < steps - 1:
+                send_row(step + 1, fields.at[step], i)
+            else:
+                for k in peers:
+                    to_member(step, k, i).start()
+
+        def pause():
+            if step == steps - 1:
+                for r in range(steps, len(rounds)):
+                    reached(r)
+                    if r + 1 < len(rounds):
+                        reach_out(r + 1)
+
+        convolve(win, wout, step, own, act, advance, pause)
         if step < steps - 1:
-            halo_start(step + 1, fields.at[step])
-        if step == steps - 1:
-            for r in range(steps, len(rounds)):
-                reached(r)
-                if r + 1 < len(rounds):
-                    reach_out(r + 1)
-        for i in range(rows):
-            for k in peers:
-                to_member(step, k, i).start()
-
+            for i in range(rows):
+                for k in peers:
+                    to_member(step, k, i).start()
+
+    for step in range(steps):
+        slopes_of(step)
     arrive(4)
     arrive(5)
     partial = jnp.zeros((8, cols), F32)
     for step in range(steps):
-        for i in range(rows):
+        for i in reversed(range(rows)):
             landed = others.at[step, :, i]
             pltpu.make_async_copy(landed, landed, other_recv.at[step, i]).wait()
             partial = partial + loss_terms(step, i)
             if step == steps - 1:
                 grads[step, i] = loss_grad[step, i]
-                if i < 2:
-                    slow_start(steps, grads.at[step], (i,))
-                if rows - 1 - i < 2:
-                    to_fast(steps, grads.at[step], rows - 1 - i).start()
+                send_row(steps, grads.at[step], i)
 
     me = me_m * bands + me_l
     parts[me] = jnp.sum(partial, axis=0, keepdims=True)
-    for n in range(1, members * bands):
-        pltpu.make_async_remote_copy(
-            src_ref=parts.at[me], dst_ref=parts.at[me], send_sem=part_send.at[0], recv_sem=part_recv.at[0],
-            device_id={"member": lax.rem(me_m + n // bands, members), "lat": lax.rem(me_l + n % bands, bands)},
-            device_id_type=MESH).start()
 
     for step in range(steps - 1, -1, -1):
         n = 2 * steps - 1 - step
         own = grads.at[step]
-        if step < steps - 1:
-            for i in range(rows):
-                grads[step, i] = grads[step + 1, i] + change[i] + loss_grad[step, i]
-            halo_start(n, own)
-        own_part(woutb, own)
-        change = convolve(woutb, winb, n, own, functools.partial(unbend, step))
-
-    for i in range(rows):
-        grad_ref[mirrored(i, rows - 1)] = grads[0, i] + change[i]
+
+        def retreat(i, change):
+            if step > 0:
+                grads[step - 1, i] = grads[step, i] + change + loss_grad[step - 1, i]
+                send_row(n + 1, grads.at[step - 1], i)
+            else:
+                grad_ref[mirror[i]] = grads[0, i] + change
+
+        act = functools.partial(unbend, step)
+        own_part(woutb, winb, own, act)
+        if step == steps - 1:
+            for k in range(1, members * bands):
+                pltpu.make_async_remote_copy(
+                    src_ref=parts.at[me], dst_ref=parts.at[me], send_sem=part_send.at[0], recv_sem=part_recv.at[0],
+                    device_id={"member": lax.rem(me_m + k // bands, members), "lat": lax.rem(me_l + k % bands, bands)},
+                    device_id_type=MESH).start()
+        convolve(woutb, winb, n, own, act, retreat)
+
     sent = parts.at[0:members * bands - 1]
     pltpu.make_async_copy(sent, sent, part_recv.at[0]).wait()
     total = jnp.sum(parts[...], axis=0)
@@ -422,8 +458,8 @@
             pltpu.VMEM((steps, rows, chans, cols), F32),
             pltpu.VMEM((steps, rows, chans, cols), F32),
             pltpu.VMEM((3, 2 * hidden, depth), BF16),
-            pltpu.VMEM((2 * taps, deep), BF16),
-            pltpu.VMEM((2 * taps, deep), BF16),
+            pltpu.VMEM((3, 2 * taps, hidden), BF16),
+            pltpu.VMEM((3, 2 * taps, hidden), BF16),
             pltpu.VMEM((3, 2 * hidden, depth), BF16),
             pltpu.VMEM((depth, hidden), F32),
             pltpu.VMEM(((rows + 4) * depth, cols), BF16),
@@ -432,7 +468,9 @@
             pltpu.VMEM(((rows + 2) * hidden, cols), BF16),
             pltpu.VMEM((rows + 2, hidden, cols), F32),
             pltpu.VMEM((steps, rows + 2, hidden, cols), F32),
-            pltpu.VMEM((rows, taps, cols), F32),
+            pltpu.VMEM((steps, rows + 2, hidden, cols), F32),
+            pltpu.VMEM((2, taps, cols), F32),
+            pltpu.VMEM((2, taps, cols), F32),
             pltpu.VMEM((steps, rows, chans, cols), F32),
             pltpu.VMEM((hidden, cols), F32),
             dma((2,)), dma((2 * steps, 2)), dma((2 * steps,)),

time: 26.8 us -> 26.3 us (0.981); the launches traced: 26.3 us -> 26.1 us
  no operation moved by 1% of the time
where the time goes in v4:
time: 26.3 us; the launch traced here: 26.1 us
  Pallas kernels  25.5 us (97%)
  between operations  0.64 us (2%)
    pallas_call x1, Pallas kernels, on_device(): pl.pallas_call(functools.partial(kernel, members, bands), out_shape=(pltp...  24.8 us
    pallas_call x1, Pallas kernels, on_device(): pl.pallas_call(deliver, out_shape=(jax.ShapeDtypeStruct((rows, chans, col...  0.66 us

profile of v4, /device:TPU:1, one launch (start us, length us, event | category | flops | bytes accessed | tf_op | source)
XLA Modules:
  0.0 26.1 jit_solution(4229411562210773375)
XLA Ops:
  0.6 24.8 %shard_map.77 = (f32[2,80,128]{2,1,0:T(8,128)S(1)}, f32[8,128]{1,0:T(8,128)S(1)}) custom-call(f32[2,80,128]{2,1,0:T(8,128)} %bitcast.7, f32[2,2,80,128]{3,2,1,0:T(8,128)} %target_hbm.1, f32[1,2]{1,0:T(1,128)} %bitcast.9, f32[720,256]{1,0:T(8,128)} %bitcast.6, f32[80,2304]{1,0:T(8,128)} %w_out_hbm.1, f32[1,256]{1,0:T(1,128)} %bitcast.8), custom_call_target="tpu_custom_call" | custom-call | tf_op jit(solution)/shard_map/pallas_call | solution.py:442
  25.5 0.7 %shard_map.78 = (f32[2,80,128]{2,1,0:T(8,128)}, f32[1,1]{1,0:T(1,128)}) custom-call(f32[2,80,128]{2,1,0:T(8,128)S(1)} %get-tuple-element.6.grad_vmem, f32[8,128]{1,0:T(8,128)S(1)} %get-tuple-element.7.loss_vmem), custom_call_target="tpu_custom_call" | custom-call | tf_op jit(solution)/shard_map/pallas_call | solution.py:488

commit v5 on v4

--- a/solution.py
+++ b/solution.py
@@ -40,7 +40,7 @@
     x_hbm, target_hbm, lat_hbm, w_in_hbm, w_out_hbm, bias_hbm,
     grad_ref, loss_ref,
     x_ref, target_ref, lat_ref, w_in_ref, w_out_ref, bias_ref, fetch_sem,
-    halo, others, parts, fields, grads,
+    halo, everyone, parts, fields, grads,
     win, winb, wout, woutb, tall, s_high, s_low, h_high, h_low, before, slope, bent, narrowed, edge, loss_grad, bias,
     halo_send, slow_recv, fast_recv, other_send, other_recv, part_send, part_recv, reach,
 ):
@@ -126,7 +126,7 @@
 
     def to_member(step, k, i):
         return pltpu.make_async_remote_copy(
-            src_ref=fields.at[step, i], dst_ref=others.at[step, k - 1, i],
+            src_ref=everyone.at[step, me_m, i], dst_ref=everyone.at[step, me_m, i],
             send_sem=other_send.at[0], recv_sem=other_recv.at[step, i],
             device_id={"member": peer(k)}, device_id_type=MESH)
 
@@ -280,7 +280,7 @@
             for i in range(2):
                 edge[i] = narrow_line(slim, 1 - i, 1)
 
-    def convolve(wide, slim, n, own, act, finish, pause=lambda: None):
+    def convolve(wide, slim, n, own, act, finish):
         pltpu.make_async_copy(halo.at[n, 1], halo.at[n, 1], fast_recv.at[n]).wait()
         for far in range(2):
             put_line(rows + 2 + far, halo[n, 1, far])
@@ -293,7 +293,6 @@
                 narrowed[i] = line
             else:
                 finish(i, collect(line))
-        pause()
 
         @pl.when(jnp.logical_not(has_slow))
         def _():
@@ -315,24 +314,34 @@
     def fold(value):
         return sum(value[8 * i:8 * i + 8] for i in range(chans // 8))
 
-    def loss_terms(step, i):
-        weight = jnp.where(odd == 1, lat_ref[0:1, rows - 1 - i:rows - i], lat_ref[0:1, i:i + 1])
+    def row_weight(i):
+        return jnp.where(odd == 1, lat_ref[0:1, rows - 1 - i:rows - i], lat_ref[0:1, i:i + 1])
+
+    def apart(spread):
+        square = spread * spread + smooth_width * smooth_width
+        return square, lax.rsqrt(square)
+
+    def loss_slopes(step, i):
         mine = fields[step, i]
         error = mine - target_ref[step, i]
-        square = error * error + smooth_width * smooth_width
-        inverse = lax.rsqrt(square)
-        direct = square * inverse
-        gradient = error * inverse
-        summed = jnp.full(mine.shape, smooth_width, F32)
+        gradient = error * apart(error)[1]
         slopes = jnp.zeros_like(mine)
         for k in range(1, members):
-            spread = mine - others[step, k - 1, i]
-            square = spread * spread + smooth_width * smooth_width
-            inverse = lax.rsqrt(square)
-            summed = summed + square * inverse
-            slopes = slopes + spread * inverse
-        loss_grad[step, i] = weight * (gradient - slopes / (members - 1))
-        return weight * fold(direct - summed / (2.0 * (members - 1)))
+            spread = mine - everyone[step, lax.rem(me_m + k, members), i]
+            slopes = slopes + spread * apart(spread)[1]
+        return row_weight(i) * (gradient - slopes / (members - 1))
+
+    def band_loss(step, i):
+        states = [everyone[step, m, i] for m in range(members)]
+        direct = jnp.zeros_like(states[0])
+        pairs = jnp.full(direct.shape, 0.5 * members * smooth_width, F32)
+        for m, state in enumerate(states):
+            square, inverse = apart(state - target_ref[step, i])
+            direct = direct + square * inverse
+            for other in states[m + 1:]:
+                square, inverse = apart(state - other)
+                pairs = pairs + square * inverse
+        return row_weight(i) * fold(direct - pairs / (members - 1))
 
     for step in range(steps):
         own = x_ref if step == 0 else fields.at[step - 1]
@@ -349,21 +358,16 @@
                 reach_out(step + 1)
 
         def advance(i, change):
-            fields[step, i] = own[i] + change
+            state = own[i] + change
+            fields[step, i] = state
+            everyone[step, me_m, i] = state
             if step < steps - 1:
                 send_row(step + 1, fields.at[step], i)
             else:
                 for k in peers:
                     to_member(step, k, i).start()
 
-        def pause():
-            if step == steps - 1:
-                for r in range(steps, len(rounds)):
-                    reached(r)
-                    if r + 1 < len(rounds):
-                        reach_out(r + 1)
-
-        convolve(win, wout, step, own, act, advance, pause)
+        convolve(win, wout, step, own, act, advance)
         if step < steps - 1:
             for i in range(rows):
                 for k in peers:
@@ -371,20 +375,24 @@
 
     for step in range(steps):
         slopes_of(step)
+    for r in range(steps, len(rounds)):
+        reached(r)
+        if r + 1 < len(rounds):
+            reach_out(r + 1)
     arrive(4)
     arrive(5)
     partial = jnp.zeros((8, cols), F32)
     for step in range(steps):
         for i in reversed(range(rows)):
-            landed = others.at[step, :, i]
+            landed = everyone.at[step, 0:members - 1, i]
             pltpu.make_async_copy(landed, landed, other_recv.at[step, i]).wait()
-            partial = partial + loss_terms(step, i)
-            if step == steps - 1:
-                grads[step, i] = loss_grad[step, i]
+            if step < steps - 1:
+                loss_grad[step, i] = loss_slopes(step, i)
+            else:
+                grads[step, i] = loss_slopes(step, i)
                 send_row(steps, grads.at[step], i)
-
-    me = me_m * bands + me_l
-    parts[me] = jnp.sum(partial, axis=0, keepdims=True)
+            if step < steps - 1 or i > 0:
+                partial = partial + band_loss(step, i)
 
     for step in range(steps - 1, -1, -1):
         n = 2 * steps - 1 - step
@@ -400,20 +408,22 @@
         act = functools.partial(unbend, step)
         own_part(woutb, winb, own, act)
         if step == steps - 1:
-            for k in range(1, members * bands):
+            partial = partial + band_loss(step, 0)
+            parts[me_l] = jnp.sum(partial, axis=0, keepdims=True)
+            for k in range(1, bands):
                 pltpu.make_async_remote_copy(
-                    src_ref=parts.at[me], dst_ref=parts.at[me], send_sem=part_send.at[0], recv_sem=part_recv.at[0],
-                    device_id={"member": lax.rem(me_m + k // bands, members), "lat": lax.rem(me_l + k % bands, bands)},
-                    device_id_type=MESH).start()
+                    src_ref=parts.at[me_l], dst_ref=parts.at[me_l], send_sem=part_send.at[0], recv_sem=part_recv.at[0],
+                    device_id={"lat": lax.rem(me_l + k, bands)}, device_id_type=MESH).start()
         convolve(woutb, winb, n, own, act, retreat)
 
-    sent = parts.at[0:members * bands - 1]
+    sent = parts.at[0:bands - 1]
     pltpu.make_async_copy(sent, sent, part_recv.at[0]).wait()
     total = jnp.sum(parts[...], axis=0)
     count = members * steps * rows * bands * chans * cols
     loss_ref[...] = jnp.full(loss_ref.shape, jnp.sum(total) / count, F32)
     pltpu.make_async_copy(sent, sent, part_send.at[0]).wait()
-    pltpu.make_async_copy(others, others, other_send.at[0]).wait()
+    landed = everyone.at[:, 0:members - 1]
+    pltpu.make_async_copy(landed, landed, other_send.at[0]).wait()
     pltpu.make_async_copy(halo.at[:, 1], halo.at[:, 1], halo_send.at[1]).wait()
 
     @pl.when(has_slow)
@@ -453,8 +463,8 @@
             pltpu.VMEM((1, hidden), F32),
             dma((6,)),
             pltpu.VMEM((2 * steps, 2, 2, chans, cols), F32),
-            pltpu.VMEM((steps, members - 1, rows, chans, cols), F32),
-            pltpu.VMEM((members * bands, 1, cols), F32),
+            pltpu.VMEM((steps, members, rows, chans, cols), F32),
+            pltpu.VMEM((bands, 1, cols), F32),
             pltpu.VMEM((steps, rows, chans, cols), F32),
             pltpu.VMEM((steps, rows, chans, cols), F32),
             pltpu.VMEM((3, 2 * hidden, depth), BF16),
@@ -471,7 +481,7 @@
             pltpu.VMEM((steps, rows + 2, hidden, cols), F32),
             pltpu.VMEM((2, taps, cols), F32),
             pltpu.VMEM((2, taps, cols), F32),
-            pltpu.VMEM((steps, rows, chans, cols), F32),
+            pltpu.VMEM((steps - 1, rows, chans, cols), F32),
             pltpu.VMEM((hidden, cols), F32),
             dma((2,)), dma((2 * steps, 2)), dma((2 * steps,)),
             dma((1,)), dma((steps, rows)),

time: 26.3 us -> 25.7 us (0.977)
  Pallas kernels: 25.5 us -> 24.9 us
    pallas_call x1, Pallas kernels: 24.8 us -> 24.3 us  [on_device(): pl.pallas_call(functools.partial(kernel, members, bands), out_shape=(pltp...]
where the time goes in v5:
time: 25.7 us; the launch traced here: 25.6 us
  Pallas kernels  24.9 us (97%)
  between operations  0.64 us (2%)
    pallas_call x1, Pallas kernels, on_device(): pl.pallas_call(functools.partial(kernel, members, bands), out_shape=(pltp...  24.3 us
    pallas_call x1, Pallas kernels, on_device(): pl.pallas_call(deliver, out_shape=(jax.ShapeDtypeStruct((rows, chans, col...  0.66 us

profile of v5, /device:TPU:1, one launch (start us, length us, event | category | flops | bytes accessed | tf_op | source)
XLA Modules:
  0.0 25.6 jit_solution(594276075654564943)
XLA Ops:
  0.6 24.3 %shard_map.77 = (f32[2,80,128]{2,1,0:T(8,128)S(1)}, f32[8,128]{1,0:T(8,128)S(1)}) custom-call(f32[2,80,128]{2,1,0:T(8,128)} %bitcast.7, f32[2,2,80,128]{3,2,1,0:T(8,128)} %target_hbm.1, f32[1,2]{1,0:T(1,128)} %bitcast.9, f32[720,256]{1,0:T(8,128)} %bitcast.6, f32[80,2304]{1,0:T(8,128)} %w_out_hbm.1, f32[1,256]{1,0:T(1,128)} %bitcast.8), custom_call_target="tpu_custom_call" | custom-call | tf_op jit(solution)/shard_map/pallas_call | solution.py:452
  24.9 0.7 %shard_map.78 = (f32[2,80,128]{2,1,0:T(8,128)}, f32[1,1]{1,0:T(1,128)}) custom-call(f32[2,80,128]{2,1,0:T(8,128)S(1)} %get-tuple-element.6.grad_vmem, f32[8,128]{1,0:T(8,128)S(1)} %get-tuple-element.7.loss_vmem), custom_call_target="tpu_custom_call" | custom-call | tf_op jit(solution)/shard_map/pallas_call | solution.py:498

commit v6 on v5

--- a/solution.py
+++ b/solution.py
@@ -148,7 +148,7 @@
 
     arrive(0)
     pl.semaphore_wait(barrier, members + has_slow.astype(jnp.int32))
-    for i in range(rows):
+    for i in reversed(range(rows)):
         send_row(0, x_ref, i)
     reach_out(0)
 
@@ -215,23 +215,24 @@
                 sums[t - a] = line if t - a not in sums else sums[t - a] + line
         return sums
 
-    def half(weights, a, high, low):
-        both = jnp.concatenate([high, low], axis=1)
+    def half(weights, terms, pieces=2):
         size = weights.shape[1] // 2
-        middle = -(-size // 32) * 16
+        edges = [0] + [-(-size * p // (16 * pieces)) * 16 for p in range(1, pieces)] + [size]
         lines = []
-        for first, last in ((0, middle), (middle, size)):
-            line = dot(weights[a, first:last, :], both) + dot(weights[a, size + first:size + last, :], both)
+        for first, last in zip(edges, edges[1:]):
+            line = sum(
+                dot(weights[a, at + first:at + last, :], both) for a, both in terms for at in (0, size))
             lines.append(line[:, 0:cols] + line[:, cols:2 * cols])
         return jnp.concatenate(lines, axis=0)
 
-    def widen_line(weights, a, t):
-        at = t * depth
-        return half(weights, a, s_high[at:at + depth, :], s_low[at:at + depth, :])
-
-    def narrow_line(weights, a, j):
-        at = j * hidden
-        return half(weights, a, h_high[at:at + hidden, :], h_low[at:at + hidden, :])
+    def beside(high, low, size, t):
+        return jnp.concatenate([high[t * size:(t + 1) * size, :], low[t * size:(t + 1) * size, :]], axis=1)
+
+    def widen_line(weights, a, t, pieces=2):
+        return half(weights, [(a, beside(s_high, s_low, depth, t))], pieces)
+
+    def narrow_line(weights, *taps_of):
+        return half(weights, [(a, beside(h_high, h_low, hidden, j)) for a, j in taps_of])
 
     def collect(total):
         return sum(shifted(total[b * chans:(b + 1) * chans], b) for b in range(3))
@@ -278,7 +279,7 @@
         def _():
             act(1, before[1])
             for i in range(2):
-                edge[i] = narrow_line(slim, 1 - i, 1)
+                edge[i] = narrow_line(slim, (1 - i, 1))
 
     def convolve(wide, slim, n, own, act, finish):
         pltpu.make_async_copy(halo.at[n, 1], halo.at[n, 1], fast_recv.at[n]).wait()
@@ -308,8 +309,8 @@
             put_line(1, halo[n, 0, 0])
             act(1, before[1] + widen_line(wide, 0, 1))
             act(0, before[0] + widen_line(wide, 1, 1))
-            finish(1, collect(narrowed[1] + narrow_line(slim, 0, 1)))
-            finish(0, collect(narrowed[0] + narrow_line(slim, 1, 1) + narrow_line(slim, 0, 0)))
+            finish(1, collect(narrowed[1] + narrow_line(slim, (0, 1))))
+            finish(0, collect(narrowed[0] + narrow_line(slim, (1, 1), (0, 0))))
 
     def fold(value):
         return sum(value[8 * i:8 * i + 8] for i in range(chans // 8))
@@ -350,8 +351,6 @@
             narrow_weights()
         act = functools.partial(bend, step)
         own_part(win, wout, own, act)
-        if step > 0:
-            back_weights()
         if step < len(rounds):
             reached(step)
             if step + 1 < len(rounds):
@@ -373,6 +372,7 @@
                 for k in peers:
                     to_member(step, k, i).start()
 
+    back_weights()
     for step in range(steps):
         slopes_of(step)
     for r in range(steps, len(rounds)):

time: 25.7 us -> 25.4 us (0.988)
  Pallas kernels: 24.9 us -> 24.6 us
    pallas_call x1, Pallas kernels: 24.3 us -> 24 us  [on_device(): pl.pallas_call(functools.partial(kernel, members, bands), out_shape=(pltp...]
where the time goes in v6:
time: 25.4 us; the launch traced here: 25.3 us
  Pallas kernels  24.6 us (97%)
  between operations  0.64 us (3%)
    pallas_call x1, Pallas kernels, on_device(): pl.pallas_call(functools.partial(kernel, members, bands), out_shape=(pltp...  24 us
    pallas_call x1, Pallas kernels, on_device(): pl.pallas_call(deliver, out_shape=(jax.ShapeDtypeStruct((rows, chans, col...  0.66 us

profile of v6, /device:TPU:1, one launch (start us, length us, event | category | flops | bytes accessed | tf_op | source)
XLA Modules:
  0.0 25.3 jit_solution(10362564933425409450)
XLA Ops:
  0.6 24.0 %shard_map.77 = (f32[2,80,128]{2,1,0:T(8,128)S(1)}, f32[8,128]{1,0:T(8,128)S(1)}) custom-call(f32[2,80,128]{2,1,0:T(8,128)} %bitcast.7, f32[2,2,80,128]{3,2,1,0:T(8,128)} %target_hbm.1, f32[1,2]{1,0:T(1,128)} %bitcast.9, f32[720,256]{1,0:T(8,128)} %bitcast.6, f32[80,2304]{1,0:T(8,128)} %w_out_hbm.1, f32[1,256]{1,0:T(1,128)} %bitcast.8), custom_call_target="tpu_custom_call" | custom-call | tf_op jit(solution)/shard_map/pallas_call | solution.py:452
  24.6 0.7 %shard_map.78 = (f32[2,80,128]{2,1,0:T(8,128)}, f32[1,1]{1,0:T(1,128)}) custom-call(f32[2,80,128]{2,1,0:T(8,128)S(1)} %get-tuple-element.6.grad_vmem, f32[8,128]{1,0:T(8,128)S(1)} %get-tuple-element.7.loss_vmem), custom_call_target="tpu_custom_call" | custom-call | tf_op jit(solution)/shard_map/pallas_call | solution.py:498

commit v7 on v6

--- a/solution.py
+++ b/solution.py
@@ -208,8 +208,9 @@
         for a, lines in parts:
             high = joined(s_high, depth, lines)
             low = joined(s_low, depth, lines)
-            both = dot(weights[a], high)
-            total = both[0:hidden] + both[hidden:2 * hidden] + dot(weights[a, 0:hidden, :], low)
+            total = jnp.concatenate([
+                dot(weights[a, at:at + hidden // 2, :], high) + dot(weights[a, hidden + at:hidden + at + hidden // 2, :], high)
+                + dot(weights[a, at:at + hidden // 2, :], low) for at in (0, hidden // 2)], axis=0)
             for n, t in enumerate(lines):
                 line = total[:, n * cols:(n + 1) * cols]
                 sums[t - a] = line if t - a not in sums else sums[t - a] + line
@@ -285,11 +286,16 @@
         pltpu.make_async_copy(halo.at[n, 1], halo.at[n, 1], fast_recv.at[n]).wait()
         for far in range(2):
             put_line(rows + 2 + far, halo[n, 1, far])
-        sums = widen(wide, [(2, (rows + 2, rows + 3)), (1, (rows + 2,))])
+        sums = widen(wide, [(2, (rows + 2, rows + 3))])
+        sums[rows + 1] = sums[rows + 1] + widen_line(wide, 1, rows + 2)
         for j in range(2, rows + 2):
             act(j, before[j] + sums[j] if j in sums else before[j])
         ready = [(a, [i for i in range(rows) if i + a >= 2]) for a in (2, 1, 0)]
-        for i, line in narrow(slim, [part for part in ready if part[1]]).items():
+        outs = narrow(slim, [part for part in ready if len(part[1]) > 1])
+        for a, alone in ready:
+            if len(alone) == 1:
+                outs[alone[0]] = outs[alone[0]] + narrow_line(slim, (a, alone[0] + a))
+        for i, line in outs.items():
             if i < 2:
                 narrowed[i] = line
             else:
@@ -307,9 +313,12 @@
             before[0] += widen_line(wide, 0, 0)
             to_slow(n, own, 0).wait_recv()
             put_line(1, halo[n, 0, 0])
-            act(1, before[1] + widen_line(wide, 0, 1))
-            act(0, before[0] + widen_line(wide, 1, 1))
-            finish(1, collect(narrowed[1] + narrow_line(slim, (0, 1))))
+            line1 = before[1] + widen_line(wide, 0, 1)
+            line0 = before[0] + widen_line(wide, 1, 1)
+            act(1, line1)
+            out1 = collect(narrowed[1] + narrow_line(slim, (0, 1)))
+            act(0, line0)
+            finish(1, out1)
             finish(0, collect(narrowed[0] + narrow_line(slim, (1, 1), (0, 0))))
 
     def fold(value):

time: 25.4 us -> 25.3 us (level)
  no operation moved by 1% of the time
where the time goes in v7:
time: 25.3 us; the launch traced here: 25.2 us
  Pallas kernels  24.5 us (97%)
  between operations  0.64 us (3%)
    pallas_call x1, Pallas kernels, on_device(): pl.pallas_call(functools.partial(kernel, members, bands), out_shape=(pltp...  23.9 us
    pallas_call x1, Pallas kernels, on_device(): pl.pallas_call(deliver, out_shape=(jax.ShapeDtypeStruct((rows, chans, col...  0.66 us

profile of v7, /device:TPU:1, one launch (start us, length us, event | category | flops | bytes accessed | tf_op | source)
XLA Modules:
  0.0 25.2 jit_solution(6474225598250662490)
XLA Ops:
  0.6 23.9 %shard_map.77 = (f32[2,80,128]{2,1,0:T(8,128)S(1)}, f32[8,128]{1,0:T(8,128)S(1)}) custom-call(f32[2,80,128]{2,1,0:T(8,128)} %bitcast.7, f32[2,2,80,128]{3,2,1,0:T(8,128)} %target_hbm.1, f32[1,2]{1,0:T(1,128)} %bitcast.9, f32[720,256]{1,0:T(8,128)} %bitcast.6, f32[80,2304]{1,0:T(8,128)} %w_out_hbm.1, f32[1,256]{1,0:T(1,128)} %bitcast.8), custom_call_target="tpu_custom_call" | custom-call | tf_op jit(solution)/shard_map/pallas_call | solution.py:461
  24.5 0.7 %shard_map.78 = (f32[2,80,128]{2,1,0:T(8,128)}, f32[1,1]{1,0:T(1,128)}) custom-call(f32[2,80,128]{2,1,0:T(8,128)S(1)} %get-tuple-element.6.grad_vmem, f32[8,128]{1,0:T(8,128)S(1)} %get-tuple-element.7.loss_vmem), custom_call_target="tpu_custom_call" | custom-call | tf_op jit(solution)/shard_map/pallas_call | solution.py:507

commit v8 on v7

--- a/solution.py
+++ b/solution.py
@@ -222,8 +222,10 @@
         lines = []
         for first, last in zip(edges, edges[1:]):
             line = sum(
-                dot(weights[a, at + first:at + last, :], both) for a, both in terms for at in (0, size))
-            lines.append(line[:, 0:cols] + line[:, cols:2 * cols])
+                dot(jnp.concatenate([weights[a, at + first:at + last, :] for at in (0, size)], axis=0), both)
+                for a, both in terms)
+            line = line[:, 0:cols] + line[:, cols:2 * cols]
+            lines.append(line[0:last - first] + line[last - first:])
         return jnp.concatenate(lines, axis=0)
 
     def beside(high, low, size, t):

time: 25.3 us -> 25.4 us (level)
  no operation moved by 1% of the time
where the time goes in v8:
time: 25.4 us; the launch traced here: 25.2 us
  Pallas kernels  24.6 us (97%)
  between operations  0.64 us (3%)
    pallas_call x1, Pallas kernels, on_device(): pl.pallas_call(functools.partial(kernel, members, bands), out_shape=(pltp...  23.9 us
    pallas_call x1, Pallas kernels, on_device(): pl.pallas_call(deliver, out_shape=(jax.ShapeDtypeStruct((rows, chans, col...  0.66 us

profile of v8, /device:TPU:1, one launch (start us, length us, event | category | flops | bytes accessed | tf_op | source)
XLA Modules:
  0.0 25.2 jit_solution(237478053751095973)
XLA Ops:
  0.6 23.9 %shard_map.77 = (f32[2,80,128]{2,1,0:T(8,128)S(1)}, f32[8,128]{1,0:T(8,128)S(1)}) custom-call(f32[2,80,128]{2,1,0:T(8,128)} %bitcast.7, f32[2,2,80,128]{3,2,1,0:T(8,128)} %target_hbm.1, f32[1,2]{1,0:T(1,128)} %bitcast.9, f32[720,256]{1,0:T(8,128)} %bitcast.6, f32[80,2304]{1,0:T(8,128)} %w_out_hbm.1, f32[1,256]{1,0:T(1,128)} %bitcast.8), custom_call_target="tpu_custom_call" | custom-call | tf_op jit(solution)/shard_map/pallas_call | solution.py:463
  24.6 0.7 %shard_map.78 = (f32[2,80,128]{2,1,0:T(8,128)}, f32[1,1]{1,0:T(1,128)}) custom-call(f32[2,80,128]{2,1,0:T(8,128)S(1)} %get-tuple-element.6.grad_vmem, f32[8,128]{1,0:T(8,128)S(1)} %get-tuple-element.7.loss_vmem), custom_call_target="tpu_custom_call" | custom-call | tf_op jit(solution)/shard_map/pallas_call | solution.py:509
